TPU v7x, 512 devices: a whole 4x4x16 slice. The times are simulated.
512 devices in a mesh: rep: 4 (over y), exp: 128 (over x, z, core).
Axes of the slice: x: 4, y: 4, z: 16, core: 2. Of those that a mesh axis runs over, the one named last changes fastest.
Arguments:
- tokens: bfloat16 [16384, 3584], P(('rep', 'exp')), parts along dimension 0, may hold values from -6 to 6
- expert_ids: int32 [16384, 8], P(('rep', 'exp')), parts along dimension 0, may hold values from 0 to 383, all different within a row; in each aligned block of 32 rows (0 to 31, 32 to 63, ...) at most 2 rows name the same one
- gate_scores: float32 [16384, 8], P(('rep', 'exp')), parts along dimension 0, may hold values from 0.02 to 0.4
- gate_weight: bfloat16 [3584, 16384], P(None, 'exp'), may hold values from -0.09375 to 0.09375
- up_weight: bfloat16 [3584, 16384], P(None, 'exp'), may hold values from -0.09375 to 0.09375
- down_weight: bfloat16 [16384, 3584], P('exp'), may hold values from -0.125 to 0.125
Outputs:
- combined: bfloat16 [16384, 3584], P(('rep', 'exp')), parts along dimension 0
- expert_load: float32 [1536], P('rep'), parts along dimension 0
There are 4 independent parts, one for each index of `rep`. A program takes and returns all parts, laid end to end along the dimension named above; an argument that names none is the same for every part. Nothing has to cross between parts.
Inputs may be any that keep to these rules, and one draw needn't show every extreme that they name: `expert_ids`: each row names 8 different experts. Among the rows of one device no expert is named by more than 2 rows, a bound that some block reaches.
All inputs are finite; a program needn't handle non-finite values.
Results may differ from a plain program's by a relative error of at most 0.0057.
Values may be sent and summed in bfloat16 or wider, within the bound.
No kernel may reach another device: no remote copies, remote signals or barrier semaphores. Data moves between devices by JAX's collectives and lax.ppermute only.
A program may use at most 64 MiB of HBM per device.

v0:
```python
import jax
import jax.numpy as jnp
from jax import lax
from jax.sharding import PartitionSpec as P

FF = 2048
EXPERTS_ALL = 384
EXPERTS = 8
CAP = 2


def expert_rows(arrived, gate_weight, up_weight, down_weight):
    flat_rows = arrived.reshape(-1, arrived.shape[-1])
    gate_act = jnp.dot(flat_rows, gate_weight, preferred_element_type=jnp.float32)
    up_act = jnp.dot(flat_rows, up_weight, preferred_element_type=jnp.float32)
    hidden = (jax.nn.silu(gate_act) * up_act).astype(jnp.bfloat16)
    partial_value = jnp.dot(hidden, down_weight, preferred_element_type=jnp.float32).astype(
        jnp.bfloat16
    )
    return partial_value.reshape(arrived.shape)


def shards(tokens, expert_ids, gate_scores, gate_weight, up_weight, down_weight):
    dev_count = lax.axis_size("exp")
    hid_dev = gate_weight.shape[1]
    spread = FF // hid_dev
    tok_rows = tokens.shape[0]
    feat_width = tokens.shape[1]
    matches = expert_ids[:, :, None] == jnp.arange(EXPERTS_ALL, dtype=jnp.int32)[None, None, :]
    onehot = jnp.where(matches, 1.0, 0.0).astype(jnp.float32)
    routed_mass = jnp.einsum("tk,tke->e", gate_scores, onehot, precision=lax.Precision.HIGHEST)
    expert_load = lax.psum(routed_mass, "exp")
    window_match = matches[:, :, :EXPERTS]
    win_hits = jnp.any(window_match, axis=1)
    win_gate = jnp.sum(jnp.where(window_match, gate_scores[:, :, None], 0.0), axis=1)
    position = jnp.cumsum(win_hits.astype(jnp.int32), axis=0) - 1
    slot_ids = jnp.arange(CAP, dtype=jnp.int32)
    placed = win_hits[:, :, None] & (position[:, :, None] == slot_ids[None, None, :])
    placing = placed.reshape(tok_rows, EXPERTS * CAP)
    picker = jnp.where(placing.T, 1.0, 0.0).astype(jnp.bfloat16)
    outgoing = jnp.dot(picker, tokens, preferred_element_type=jnp.float32).astype(jnp.bfloat16)
    outgoing = jnp.broadcast_to(
        outgoing.reshape(EXPERTS, 1, CAP, feat_width), (EXPERTS, spread, CAP, feat_width)
    )
    outgoing = outgoing.reshape(dev_count, CAP, feat_width)
    arrived = lax.all_to_all(outgoing, "exp", split_axis=0, concat_axis=0, tiled=True)
    returned = lax.all_to_all(
        expert_rows(arrived, gate_weight, up_weight, down_weight),
        "exp",
        split_axis=0,
        concat_axis=0,
        tiled=True,
    )
    summed = jnp.sum(returned.reshape(EXPERTS, spread, CAP, feat_width), axis=1, dtype=jnp.float32)
    summed = summed.reshape(EXPERTS * CAP, feat_width)
    weights_slot = jnp.where(placed, win_gate[:, :, None], 0.0).reshape(tok_rows, EXPERTS * CAP)
    combined = jnp.dot(weights_slot, summed, precision=lax.Precision.HIGHEST).astype(jnp.bfloat16)
    return (combined, expert_load)


def solution(mesh):
    return jax.shard_map(
        shards,
        mesh=mesh,
        in_specs=(
            P(("rep", "exp"), None),
            P(("rep", "exp"), None),
            P(("rep", "exp"), None),
            P(None, "exp"),
            P(None, "exp"),
            P("exp", None),
        ),
        out_specs=(P(("rep", "exp"), None), P("rep")),
        check_vma=False,
    )
```

profile of v0, /device:TPU:24, one launch (start us, length us, event | category | flops | bytes accessed | tf_op | source)
XLA Modules:
  0.0 457.5 jit_solution(18036229864362332462)
XLA Ops:
  0.6 0.0 copy-start
  0.7 0.1 eq.45
  0.7 1.0 iota_compare_fusion
  1.8 0.1 copy.23
  1.8 0.1 reduce_window_sum.11
  1.9 0.1 copy.24
  2.0 1.2 convolution_convert_fusion.1
  3.2 0.9 broadcast_in_dim.61
  4.2 107.4 %all_to_all.10 = bf16[128,2,3584]{2,1,0:T(2,128)(2,1)} all-to-all(bf16[128,2,3584]{2,1,0:T(2,128)(2,1)S(1)} %bitcast.21), channel_id=1, replica_groups=mesh['rep'=4,'exp'=128] {'exp'}, dimensions={0} | all-to-all | bytes 3670016 | tf_op jit(solution)/shard_map/all_to_all | solution.py:46
  111.6 4.1 reshape.38
  115.7 1.8 fusion.25
  117.5 0.0 copy-done
  117.5 3.6 convolution_convert_fusion
  121.1 4.7 %reshape.39 = bf16[128,2,3584]{2,1,0:T(2,128)(2,1)} reshape(bf16[256,3584]{1,0:T(8,128)(2,1)} %convolution_convert_fusion) | data formatting | bytes 3670016 | tf_op jit(solution)/shard_map/reshape | solution.py:20
  125.8 0.0 copy-start.1
  125.8 0.0 copy-start.2
  125.8 9.0 %all-to-all-start.1 = ((bf16[128,2,3584]{2,1,0:T(2,128)(2,1)}), bf16[128,2,3584]{2,1,0:T(2,128)(2,1)S(1)}, u32[]{:S(2)}, u32[]{:S(2)}) async-start(bf16[128,2,3584]{2,1,0:T(2,128)(2,1)} %reshape.39), calls=%async_computation.1 | async-start | bytes 3670016 | tf_op jit(solution)/shard_map/all_to_all | solution.py:47
  134.8 0.0 copy-done.1
  134.8 0.0 copy-done.2
  134.8 1.5 fusion.4
  136.4 318.3 %psum.7 = f32[384]{0:T(512)} all-reduce(f32[384]{0:T(512)S(1)} %fusion.4), channel_id=1, replica_groups=mesh['rep'=4,'exp'=128] {'exp'}, use_global_device_ids=true, to_apply=%region_4.5 | all-reduce | flops 384 | bytes 3072 | tf_op jit(solution)/shard_map/psum | solution.py:32
  454.7 0.0 all-to-all-done.1
  454.7 1.5 convert_reduce_fusion
  456.2 1.3 fusion
  (10 shorter events, 0.1 us)
Async XLA Ops:
  0.6 116.8 %copy-start = (bf16[128,3584]{1,0:T(8,128)(2,1)S(1)}, bf16[128,3584]{1,0:T(8,128)(2,1)}, u32[]{:S(2)}) copy-start(bf16[128,3584]{1,0:T(8,128)(2,1)} %param.11) | copy-start | bytes 2752516
  125.8 9.0 %copy-start.1 = (s32[32,8]{0,1:T(8,128)S(1)}, s32[32,8]{0,1:T(8,128)}, u32[]{:S(2)}) copy-start(s32[32,8]{0,1:T(8,128)} %param.7) | copy-start | bytes 3076
  125.8 9.0 %copy-start.2 = (f32[32,8]{0,1:T(8,128)S(1)}, f32[32,8]{0,1:T(8,128)}, u32[]{:S(2)}) copy-start(f32[32,8]{0,1:T(8,128)} %param.8) | copy-start | bytes 3076
  125.8 328.9 %all-to-all-start.1 = ((bf16[128,2,3584]{2,1,0:T(2,128)(2,1)}), bf16[128,2,3584]{2,1,0:T(2,128)(2,1)S(1)}, u32[]{:S(2)}, u32[]{:S(2)}) async-start(bf16[128,2,3584]{2,1,0:T(2,128)(2,1)} %reshape.39), calls=%async_computation.1 | async-start | bytes 3670016 | tf_op jit(solution)/shard_map/all_to_all | solution.py:47
where the time goes:
time: 459 us; the launch traced here: 457 us
  blocking collectives  426 us (93%)
  local copies, waits for them, and re-layouts  10.1 us (2%)
  matrix products  9.37 us (2%)
  starting transfers between devices  8.97 us (2%)
    psum x1, blocking collectives, shards(): expert_load = lax.psum(routed_mass, 'exp')  318 us
    all_to_all x1, blocking collectives, shards(): lax.all_to_all(outgoing, 'exp', split_axis=0, concat_axis=0, tiled=True)  107 us
  transfers between devices with their start and end apart: 1, of which 0 were waited for; matrix products, arithmetic and copies ran while one was open for 0% of the time, Pallas kernels for 0%

commit v1 on v0

v1 whole, which is shorter than its diff:
```python
import jax
import jax.numpy as jnp
from jax import lax
from jax.sharding import PartitionSpec as P

EXPERTS_ALL = 384
EXPERTS = 8
CAP = 2
COLS, RINGS, CORES = 4, 16, 2
PAIRS = RINGS // 2


def place(col, ring, core):
    return (col * RINGS + ring) * CORES + core


def far_groups():
    groups = []
    for side in range(2):
        for core in range(CORES):
            groups.append(
                [
                    place(col, 2 * pair + (side if pair < PAIRS // 2 else 1 - side), core)
                    for col in range(COLS)
                    for pair in range(PAIRS)
                ]
            )
    return groups


FAR = far_groups()
MEMBERS = COLS * PAIRS
SPREAD = MEMBERS // EXPERTS
BESIDE = [(i, i ^ CORES) for i in range(COLS * RINGS * CORES)]
TWIN = [(i, i ^ 1) for i in range(COLS * RINGS * CORES)]
SLICE = EXPERTS_ALL // MEMBERS


def split3(v):
    a = v.astype(jnp.bfloat16)
    r = v - a.astype(jnp.float32)
    b = r.astype(jnp.bfloat16)
    c = (r - b.astype(jnp.float32)).astype(jnp.bfloat16)
    return a, b, c


def shards(tokens, expert_ids, gate_scores, gate_weight, up_weight, down_weight):
    bf, f32 = jnp.bfloat16, jnp.float32
    tok_rows, width = tokens.shape
    weights = (gate_weight, up_weight, down_weight)
    twins = tuple(lax.ppermute(w, "exp", TWIN) for w in weights)

    matches = expert_ids[:, :, None] == jnp.arange(EXPERTS_ALL, dtype=jnp.int32)[None, None, :]
    onehot = jnp.where(matches, 1.0, 0.0).astype(f32)
    mass = jnp.einsum("tk,tke->e", gate_scores, onehot, precision=lax.Precision.HIGHEST)
    window = matches[:, :, :EXPERTS]
    hits = jnp.any(window, axis=1)
    gate = jnp.sum(jnp.where(window, gate_scores[:, :, None], 0.0), axis=1)
    lower = (jnp.arange(tok_rows)[:, None] >= jnp.arange(tok_rows)[None, :]).astype(bf)
    position = jnp.dot(lower, hits.astype(bf), preferred_element_type=f32).astype(jnp.int32) - 1
    slots = jnp.arange(CAP, dtype=jnp.int32)
    placed = hits[:, :, None] & (position[:, :, None] == slots[None, None, :])
    placing = placed.reshape(tok_rows, EXPERTS * CAP)
    picker = jnp.where(placing.T, 1.0, 0.0).astype(bf)
    out = jnp.dot(picker, tokens, preferred_element_type=f32).astype(bf)
    out = jnp.broadcast_to(out.reshape(EXPERTS, 1, CAP, width), (EXPERTS, SPREAD, CAP, width))
    out = out.reshape(MEMBERS, CAP, width)
    mass = lax.psum(lax.psum(lax.psum(mass, "exp", axis_index_groups=CG), "exp", axis_index_groups=XG), "exp", axis_index_groups=ZG)
    arrived = lax.all_to_all(out, "exp", 0, 0, axis_index_groups=FAR, tiled=True)
    mine = arrived.reshape(MEMBERS * CAP, width)
    theirs = lax.ppermute(mine, "exp", BESIDE)

    def expert(rows):
        total = 0.0
        for gw, uw, dw in zip(*((w, t) for w, t in zip(weights, twins))):
            g = jnp.dot(rows, gw, preferred_element_type=f32)
            u = jnp.dot(rows, uw, preferred_element_type=f32)
            h = (jax.nn.silu(g) * u).astype(bf)
            total = total + jnp.dot(h, dw, preferred_element_type=f32)
        return total

    back = lax.ppermute(expert(theirs).astype(bf), "exp", BESIDE)
    both = (expert(mine) + back.astype(f32)).astype(bf).reshape(MEMBERS, CAP, width)
    returned = lax.all_to_all(both, "exp", 0, 0, axis_index_groups=FAR, tiled=True)
    summed = jnp.sum(returned.reshape(EXPERTS, SPREAD, CAP, width), axis=1, dtype=f32)
    scale = jnp.where(placed, gate[:, :, None], 0.0).reshape(tok_rows, EXPERTS * CAP)
    combined = jnp.dot(scale, summed.reshape(EXPERTS * CAP, width), precision=lax.Precision.HIGHEST)
    return combined.astype(bf), mass


CG = [[place(c, r, k) for k in range(CORES)] for c in range(COLS) for r in range(RINGS)]
XG = [[place(c, r, k) for c in range(COLS)] for r in range(RINGS) for k in range(CORES)]
ZG = [[place(c, r, k) for r in range(RINGS)] for c in range(COLS) for k in range(CORES)]


def solution(mesh):
    return jax.shard_map(
        shards,
        mesh=mesh,
        in_specs=(
            P(("rep", "exp"), None),
            P(("rep", "exp"), None),
            P(("rep", "exp"), None),
            P(None, "exp"),
            P(None, "exp"),
            P("exp", None),
        ),
        out_specs=(P(("rep", "exp"), None), P("rep")),
        check_vma=False,
    )
```

time: 459 us -> 143 us (0.31)
  blocking collectives: 426 us -> 44.9 us
  waiting for transfers between devices: 0.01 us -> 35.4 us
  starting transfers between devices: 8.97 us -> 41.7 us
  local copies, waits for them, and re-layouts: 10.1 us -> 3.05 us
    psum x1 -> x3, blocking collectives: 318 us -> 44.9 us  [the longest x1 31.7 us: shards(): lax.psum(lax.psum(lax.psum(mass, 'exp', axis_index_groups=CG), 'exp', axi...]
    all_to_all x1 -> x0, blocking collectives: 107 us -> none  [shards(): lax.all_to_all(outgoing, 'exp', split_axis=0, concat_axis=0, tiled=True)]
    all_to_all x1 -> x2, waiting for transfers between devices: 0.01 us -> 24.4 us  [the longest x1 24.4 us: shards(): lax.all_to_all(out, 'exp', 0, 0, axis_index_groups=FAR, tiled=True)]
    all_to_all x1 -> x2, starting transfers between devices: 8.97 us -> 25.6 us  [the longest x1 17.6 us: shards(): lax.all_to_all(out, 'exp', 0, 0, axis_index_groups=FAR, tiled=True)]
    ppermute x0 -> x5, starting transfers between devices: none -> 16.1 us  [the longest x3 6.25 us: shards(): twins = tuple((lax.ppermute(w, 'exp', TWIN) for w in weights))]
    ppermute x0 -> x5, waiting for transfers between devices: none -> 11 us  [the longest x1 6.66 us: shards(): back = lax.ppermute(expert(theirs).astype(bf), 'exp', BESIDE)]
    reshape x2, local copies, waits for them, and re-layouts: 8.8 us -> 1.12 us  [the longest x1 0.94 us: shards(): (expert(mine) + back.astype(f32)).astype(bf).reshape(MEMBERS, CAP, width)]
    dot_general x4 -> x11, matrix products: 7.85 us -> 12.3 us  [the longest x4 7.14 us: expert(): total = total + jnp.dot(h, dw, preferred_element_type=f32)]
  transfers between devices with their start and end apart: 1 -> 7, of which waited for: 0 -> 3; matrix products, arithmetic and copies ran while one was open for 0% -> 6% of each run, Pallas kernels for 0% -> 0%
where the time goes in v1:
time: 143 us; the launch traced here: 142 us
  blocking collectives  44.9 us (31%)
  starting transfers between devices  41.7 us (29%)
  waiting for transfers between devices  35.4 us (25%)
  matrix products  13.9 us (10%)
  local copies, waits for them, and re-layouts  3.05 us (2%)
  other arithmetic  2.1 us (1%)
    psum x1, blocking collectives, shards(): lax.psum(lax.psum(lax.psum(mass, 'exp', axis_index_groups=CG), 'exp', axi...  31.7 us
    all_to_all x1, waiting for transfers between devices, shards(): lax.all_to_all(out, 'exp', 0, 0, axis_index_groups=FAR, tiled=True)  24.4 us
    all_to_all x1, starting transfers between devices, shards(): lax.all_to_all(out, 'exp', 0, 0, axis_index_groups=FAR, tiled=True)  17.6 us
    psum x1, blocking collectives, shards(): lax.psum(lax.psum(mass, 'exp', axis_index_groups=CG), 'exp', axis_index_g...  10.8 us
    all_to_all x1, starting transfers between devices, shards(): lax.all_to_all(both, 'exp', 0, 0, axis_index_groups=FAR, tiled=True)  7.94 us
    dot_general x4, matrix products, expert(): total = total + jnp.dot(h, dw, preferred_element_type=f32)  7.14 us
    ppermute x1, waiting for transfers between devices, shards(): back = lax.ppermute(expert(theirs).astype(bf), 'exp', BESIDE)  6.66 us
    ppermute x3, starting transfers between devices, shards(): twins = tuple((lax.ppermute(w, 'exp', TWIN) for w in weights))  6.25 us
  transfers between devices with their start and end apart: 7, of which 3 were waited for; matrix products, arithmetic and copies ran while one was open for 6% of the time, Pallas kernels for 0%

profile of v1, /device:TPU:24, one launch (start us, length us, event | category | flops | bytes accessed | tf_op | source)
XLA Modules:
  0.0 142.0 jit_solution(13497997838877795498)
XLA Ops:
  0.6 0.0 copy-start
  0.7 0.1 eq.45
  0.7 0.9 iota_compare_fusion
  1.7 0.0 copy-start.4
  1.7 0.7 copy-done.4
  2.4 0.1 fusion.8
  2.6 0.0 copy-done
  2.6 0.2 convolution_convert_fusion
  2.8 0.0 copy-start.1
  2.9 1.0 broadcast_in_dim.63
  3.9 0.0 copy-start.2
  3.9 17.6 %all-to-all-start = ((bf16[32,2,3584]{2,1,0:T(2,128)(2,1)}), bf16[32,2,3584]{2,1,0:T(2,128)(2,1)S(1)}, u32[]{:S(2)}, u32[]{:S(2)}) async-start(bf16[32,2,3584]{2,1,0:T(2,128)(2,1)} %bitcast.1), calls=%async_computation | async-start | bytes 917504 | tf_op jit(solution)/shard_map/all_to_all | solution.py:69
  21.6 0.0 copy-done.1
  21.6 1.9 %collective-permute-start = (bf16[3584,128]{1,0:T(8,128)(2,1)S(1)}, bf16[3584,128]{1,0:T(8,128)(2,1)}, u32[]{:S(2)}, u32[]{:S(2)}) collective-permute-start(bf16[3584,128]{1,0:T(8,128)(2,1)S(1)} %copy-done.1), channel_id=1, source_target_pairs={{0,1},{1,0},{2,3},{3,2},{4,5},{5,4},{6,7},{7,6},{8,9},{9,8},{10,11... | collective-permute-start | bytes 2752520 | tf_op jit(solution)/shard_map/ppermute | solution.py:51
  23.5 24.4 %all-to-all-done = bf16[32,2,3584]{2,1,0:T(2,128)(2,1)S(1)} async-done(((bf16[32,2,3584]{2,1,0:T(2,128)(2,1)}), bf16[32,2,3584]{2,1,0:T(2,128)(2,1)S(1)}, u32[]{:S(2)}, u32[]{:S(2)}) %all-to-all-start) | async-done | bytes 458784 | tf_op jit(solution)/shard_map/all_to_all | solution.py:69
  47.9 0.2 reshape.30
  48.1 6.1 %collective-permute-start.3 = (bf16[64,3584]{1,0:T(8,128)(2,1)S(1)}, bf16[64,3584]{1,0:T(8,128)(2,1)S(1)}, u32[]{:S(2)}, u32[]{:S(2)}) collective-permute-start(bf16[64,3584]{1,0:T(8,128)(2,1)S(1)} %reshape.30), channel_id=1, source_target_pairs={{0,2},{1,3},{2,0},{3,1},{4,6},{5,7},{6,4},{7,5},{8,10},{9,11},{10,... | collective-permute-start | bytes 1376264 | tf_op jit(solution)/shard_map/ppermute | solution.py:71
  54.2 1.9 %collective-permute-start.1 = (bf16[3584,128]{1,0:T(8,128)(2,1)}, bf16[3584,128]{1,0:T(8,128)(2,1)}, u32[]{:S(2)}, u32[]{:S(2)}) collective-permute-start(bf16[3584,128]{1,0:T(8,128)(2,1)} %param.10), channel_id=1, source_target_pairs={{0,1},{1,0},{2,3},{3,2},{4,5},{5,4},{6,7},{7,6},{8,9},{9,8},{10,11... | collective-permute-start | bytes 2752520 | tf_op jit(solution)/shard_map/ppermute | solution.py:51
  56.2 0.0 copy-done.2
  56.2 2.4 %collective-permute-start.2 = (bf16[128,3584]{1,0:T(8,128)(2,1)S(1)}, bf16[128,3584]{1,0:T(8,128)(2,1)}, u32[]{:S(2)}, u32[]{:S(2)}) collective-permute-start(bf16[128,3584]{1,0:T(8,128)(2,1)S(1)} %copy-done.2), channel_id=1, source_target_pairs={{0,1},{1,0},{2,3},{3,2},{4,5},{5,4},{6,7},{7,6},{8,9},{9,8},{10,11... | collective-permute-start | bytes 2752520 | tf_op jit(solution)/shard_map/ppermute | solution.py:51
  58.6 0.3 fusion.43
  58.9 4.3 %collective-permute-done.3 = bf16[64,3584]{1,0:T(8,128)(2,1)S(1)} collective-permute-done((bf16[64,3584]{1,0:T(8,128)(2,1)S(1)}, bf16[64,3584]{1,0:T(8,128)(2,1)S(1)}, u32[]{:S(2)}, u32[]{:S(2)}) %collective-permute-start.3) | collective-permute-done | bytes 458784 | tf_op jit(solution)/shard_map/ppermute | solution.py:71
  63.2 0.3 fusion.45
  63.5 0.0 collective-permute-done
  63.5 1.5 %fusion.46 = f32[64,128]{1,0:T(8,128)S(1)} fusion(bf16[64,3584]{1,0:T(8,128)(2,1)S(1)} %collective-permute-done.3, bf16[3584,128]{1,0:T(8,128)(2,1)} %collective-permute-done), kind=kOutput, calls=%fused_computation.57 | convolution fusion | flops 58720256 | bytes 1409024 | tf_op jit(solution)/shard_map/dot_general | solution.py:76
  65.0 1.7 %fusion.20 = f32[64,3584]{1,0:T(8,128)S(1)} fusion(bf16[128,3584]{1,0:T(8,128)(2,1)S(1)} %copy-done.2, f32[64,128]{1,0:T(8,128)S(1)} %fusion.45, bf16[64,3584]{1,0:T(8,128)(2,1)S(1)} %collective-permute-done.3, bf16[3584,128]{1,0:T(8,128)(2,1)} %param.10), kind=kOutput, calls=%fused_computation.31 | convolution fusion | flops 117489664 | bytes 3244032 | tf_op jit(solution)/shard_map/dot_general | solution.py:79
  66.8 0.0 collective-permute-done.1
  66.8 0.0 collective-permute-done.2
  66.8 2.8 %fusion.2 = bf16[64,3584]{1,0:T(8,128)(2,1)} fusion(f32[64,3584]{1,0:T(8,128)S(1)} %fusion.20, bf16[128,3584]{1,0:T(8,128)(2,1)} %collective-permute-done.2, f32[64,128]{1,0:T(8,128)S(1)} %fusion.46, bf16[64,3584]{1,0:T(8,128)(2,1)S(1)} %collective-permute-done.3, bf16[3584,128]{1,0:T(8,128)(2,1)} %collective-permute-done.1), kind=kOutput, calls=%fused_computation.4 | convolution fusion | flops 117948416 | bytes 3702784 | tf_op jit(solution)/shard_map/dot_general | solution.py:79
  69.5 0.0 copy-start.3
  69.5 3.8 %collective-permute-start.4 = (bf16[64,3584]{1,0:T(8,128)(2,1)}, bf16[64,3584]{1,0:T(8,128)(2,1)}, u32[]{:S(2)}, u32[]{:S(2)}) collective-permute-start(bf16[64,3584]{1,0:T(8,128)(2,1)} %fusion.2), channel_id=1, source_target_pairs={{0,2},{1,3},{2,0},{3,1},{4,6},{5,7},{6,4},{7,5},{8,10},{9,11},{10,... | collective-permute-start | bytes 1376264 | tf_op jit(solution)/shard_map/ppermute | solution.py:82
  73.3 1.5 %fusion.44 = f32[64,128]{1,0:T(8,128)S(1)} fusion(bf16[64,3584]{1,0:T(8,128)(2,1)S(1)} %reshape.30, bf16[3584,128]{1,0:T(8,128)(2,1)} %collective-permute-done), kind=kOutput, calls=%fused_computation.55 | convolution fusion | flops 58720256 | bytes 1409024 | tf_op jit(solution)/shard_map/dot_general | solution.py:76
  74.8 0.0 copy-done.3
  74.8 0.6 fusion.7
  75.4 6.7 %collective-permute-done.4 = bf16[64,3584]{1,0:T(8,128)(2,1)} collective-permute-done((bf16[64,3584]{1,0:T(8,128)(2,1)}, bf16[64,3584]{1,0:T(8,128)(2,1)}, u32[]{:S(2)}, u32[]{:S(2)}) %collective-permute-start.4) | collective-permute-done | bytes 458784 | tf_op jit(solution)/shard_map/ppermute | solution.py:82
  82.0 2.1 %fusion.1 = bf16[64,3584]{1,0:T(8,128)(2,1)S(1)} fusion(f32[64,3584]{1,0:T(8,128)S(1)} %fusion.7, bf16[128,3584]{1,0:T(8,128)(2,1)} %collective-permute-done.2, bf16[64,3584]{1,0:T(8,128)(2,1)} %collective-permute-done.4, f32[64,128]{1,0:T(8,128)S(1)} %fusion.44, bf16[64,3584]{1,0:T(8,128)(2,1)S(1)} %reshape.30, bf16[3584,128]{1,0:T(8,128)(2,1)} %collective-permute-done.1), kind=kOutput, calls=%fused_computation.3 | convolution fusion | flops 118407168 | bytes 4161536 | tf_op jit(solution)/shard_map/dot_general | solution.py:79
  84.2 0.0 copy-start.5
  84.2 0.0 copy-start.6
  84.2 0.9 reshape.31
  85.1 7.9 %all-to-all-start.1 = ((bf16[32,2,3584]{2,1,0:T(2,128)(2,1)}), bf16[32,2,3584]{2,1,0:T(2,128)(2,1)S(1)}, u32[]{:S(2)}, u32[]{:S(2)}) async-start(bf16[32,2,3584]{2,1,0:T(2,128)(2,1)} %reshape.31), calls=%async_computation.1 | async-start | bytes 917504 | tf_op jit(solution)/shard_map/all_to_all | solution.py:84
  93.1 0.0 copy-done.5
  93.1 0.0 copy-done.6
  93.1 1.5 %fusion.9 = f32[384]{0:T(512)S(1)} fusion(f32[32,8,1]{0,2,1:T(1,128)S(1)} %bitcast.38, s32[32,8]{0,1:T(8,128)S(1)} %copy-done.5), kind=kOutput, calls=%fused_computation.16 | convolution fusion | flops 1376256 | bytes 3584 | tf_op jit(solution)/shard_map/tk,tke->e/dot_general | solution.py:55
  94.6 2.5 %psum.21 = f32[384]{0:T(512)S(1)} all-reduce(f32[384]{0:T(512)S(1)} %fusion.9), channel_id=1, replica_groups={{0,1},{2,3},{4,5},{6,7},{8,9},{10,11},{12,13},{14,15},{16,17},{18,19},{..., use_global_device_ids=true, to_apply=%region_3.4 | all-reduce | flops 384 | bytes 3072 | tf_op jit(solution)/shard_map/psum | solution.py:68
  97.1 10.8 %psum.22 = f32[384]{0:T(512)S(1)} all-reduce(f32[384]{0:T(512)S(1)} %psum.21), channel_id=1, replica_groups={{0,32,64,96},{1,33,65,97},{2,34,66,98},{3,35,67,99},{4,36,68,100},{5,37..., use_global_device_ids=true, to_apply=%region_4.5 | all-reduce | flops 384 | bytes 3072 | tf_op jit(solution)/shard_map/psum | solution.py:68
  107.8 31.7 %psum.23 = f32[384]{0:T(512)} all-reduce(f32[384]{0:T(512)S(1)} %psum.22), channel_id=1, replica_groups={{0,2,4,6,8,10,12,14,16,18,20,22,24,26,28,30},{1,3,5,7,9,11,13,15,17,19,..., use_global_device_ids=true, to_apply=%region_5.6 | all-reduce | flops 384 | bytes 3072 | tf_op jit(solution)/shard_map/psum | solution.py:68
  139.5 0.7 select_reduce_fusion
  140.3 0.0 all-to-all-done.1
  140.3 0.4 convert_reduce_fusion
  140.7 1.3 fusion.3
  (7 shorter events, 0.1 us)
Async XLA Ops:
  0.6 2.0 %copy-start = (bf16[32,3584]{1,0:T(8,128)(2,1)S(1)}, bf16[32,3584]{1,0:T(8,128)(2,1)}, u32[]{:S(2)}) copy-start(bf16[32,3584]{1,0:T(8,128)(2,1)} %param.6) | copy-start | bytes 688132
  1.7 0.7 copy-start.4
  2.8 18.7 %copy-start.1 = (bf16[3584,128]{1,0:T(8,128)(2,1)S(1)}, bf16[3584,128]{1,0:T(8,128)(2,1)}, u32[]{:S(2)}) copy-start(bf16[3584,128]{1,0:T(8,128)(2,1)} %param.9) | copy-start | bytes 2752516
  3.9 52.3 %copy-start.2 = (bf16[128,3584]{1,0:T(8,128)(2,1)S(1)}, bf16[128,3584]{1,0:T(8,128)(2,1)}, u32[]{:S(2)}) copy-start(bf16[128,3584]{1,0:T(8,128)(2,1)} %param.11) | copy-start | bytes 2752516
  3.9 44.0 %all-to-all-start = ((bf16[32,2,3584]{2,1,0:T(2,128)(2,1)}), bf16[32,2,3584]{2,1,0:T(2,128)(2,1)S(1)}, u32[]{:S(2)}, u32[]{:S(2)}) async-start(bf16[32,2,3584]{2,1,0:T(2,128)(2,1)} %bitcast.1), calls=%async_computation | async-start | bytes 917504 | tf_op jit(solution)/shard_map/all_to_all | solution.py:69
  21.6 42.0 %collective-permute-start = (bf16[3584,128]{1,0:T(8,128)(2,1)S(1)}, bf16[3584,128]{1,0:T(8,128)(2,1)}, u32[]{:S(2)}, u32[]{:S(2)}) collective-permute-start(bf16[3584,128]{1,0:T(8,128)(2,1)S(1)} %copy-done.1), channel_id=1, source_target_pairs={{0,1},{1,0},{2,3},{3,2},{4,5},{5,4},{6,7},{7,6},{8,9},{9,8},{10,11... | collective-permute-start | bytes 2752520 | tf_op jit(solution)/shard_map/ppermute | solution.py:51
  48.1 15.1 %collective-permute-start.3 = (bf16[64,3584]{1,0:T(8,128)(2,1)S(1)}, bf16[64,3584]{1,0:T(8,128)(2,1)S(1)}, u32[]{:S(2)}, u32[]{:S(2)}) collective-permute-start(bf16[64,3584]{1,0:T(8,128)(2,1)S(1)} %reshape.30), channel_id=1, source_target_pairs={{0,2},{1,3},{2,0},{3,1},{4,6},{5,7},{6,4},{7,5},{8,10},{9,11},{10,... | collective-permute-start | bytes 1376264 | tf_op jit(solution)/shard_map/ppermute | solution.py:71
  54.2 12.5 %collective-permute-start.1 = (bf16[3584,128]{1,0:T(8,128)(2,1)}, bf16[3584,128]{1,0:T(8,128)(2,1)}, u32[]{:S(2)}, u32[]{:S(2)}) collective-permute-start(bf16[3584,128]{1,0:T(8,128)(2,1)} %param.10), channel_id=1, source_target_pairs={{0,1},{1,0},{2,3},{3,2},{4,5},{5,4},{6,7},{7,6},{8,9},{9,8},{10,11... | collective-permute-start | bytes 2752520 | tf_op jit(solution)/shard_map/ppermute | solution.py:51
  56.2 10.6 %collective-permute-start.2 = (bf16[128,3584]{1,0:T(8,128)(2,1)S(1)}, bf16[128,3584]{1,0:T(8,128)(2,1)}, u32[]{:S(2)}, u32[]{:S(2)}) collective-permute-start(bf16[128,3584]{1,0:T(8,128)(2,1)S(1)} %copy-done.2), channel_id=1, source_target_pairs={{0,1},{1,0},{2,3},{3,2},{4,5},{5,4},{6,7},{7,6},{8,9},{9,8},{10,11... | collective-permute-start | bytes 2752520 | tf_op jit(solution)/shard_map/ppermute | solution.py:51
  69.5 5.3 %copy-start.3 = (bf16[3584,128]{1,0:T(8,128)(2,1)S(1)}, bf16[3584,128]{1,0:T(8,128)(2,1)}, u32[]{:S(2)}) copy-start(bf16[3584,128]{1,0:T(8,128)(2,1)} %param.10) | copy-start | bytes 2752516
  69.5 12.5 %collective-permute-start.4 = (bf16[64,3584]{1,0:T(8,128)(2,1)}, bf16[64,3584]{1,0:T(8,128)(2,1)}, u32[]{:S(2)}, u32[]{:S(2)}) collective-permute-start(bf16[64,3584]{1,0:T(8,128)(2,1)} %fusion.2), channel_id=1, source_target_pairs={{0,2},{1,3},{2,0},{3,1},{4,6},{5,7},{6,4},{7,5},{8,10},{9,11},{10,... | collective-permute-start | bytes 1376264 | tf_op jit(solution)/shard_map/ppermute | solution.py:82
  84.2 8.9 %copy-start.5 = (s32[32,8]{0,1:T(8,128)S(1)}, s32[32,8]{0,1:T(8,128)}, u32[]{:S(2)}) copy-start(s32[32,8]{0,1:T(8,128)} %param.7) | copy-start | bytes 3076
  84.2 8.9 %copy-start.6 = (f32[32,8]{0,1:T(8,128)S(1)}, f32[32,8]{0,1:T(8,128)}, u32[]{:S(2)}) copy-start(f32[32,8]{0,1:T(8,128)} %param.8) | copy-start | bytes 3076
  85.1 55.1 %all-to-all-start.1 = ((bf16[32,2,3584]{2,1,0:T(2,128)(2,1)}), bf16[32,2,3584]{2,1,0:T(2,128)(2,1)S(1)}, u32[]{:S(2)}, u32[]{:S(2)}) async-start(bf16[32,2,3584]{2,1,0:T(2,128)(2,1)} %reshape.31), calls=%async_computation.1 | async-start | bytes 917504 | tf_op jit(solution)/shard_map/all_to_all | solution.py:84

commit v2 on v1

--- a/solution.py
+++ b/solution.py
@@ -34,6 +34,7 @@
 BESIDE = [(i, i ^ CORES) for i in range(COLS * RINGS * CORES)]
 TWIN = [(i, i ^ 1) for i in range(COLS * RINGS * CORES)]
 SLICE = EXPERTS_ALL // MEMBERS
+RIDER = 128
 
 
 def split3(v):
@@ -42,6 +43,11 @@
     b = r.astype(jnp.bfloat16)
     c = (r - b.astype(jnp.float32)).astype(jnp.bfloat16)
     return a, b, c
+
+
+def riders(slices):
+    row = jnp.concatenate(split3(slices), axis=1)
+    return jnp.pad(row[:, None, :], ((0, 0), (0, CAP - 1), (0, RIDER - 3 * SLICE)))
 
 
 def shards(tokens, expert_ids, gate_scores, gate_weight, up_weight, down_weight):
@@ -65,10 +71,14 @@
     out = jnp.dot(picker, tokens, preferred_element_type=f32).astype(bf)
     out = jnp.broadcast_to(out.reshape(EXPERTS, 1, CAP, width), (EXPERTS, SPREAD, CAP, width))
     out = out.reshape(MEMBERS, CAP, width)
-    mass = lax.psum(lax.psum(lax.psum(mass, "exp", axis_index_groups=CG), "exp", axis_index_groups=XG), "exp", axis_index_groups=ZG)
+    out = jnp.concatenate([out, riders(mass.reshape(MEMBERS, SLICE))], axis=2)
     arrived = lax.all_to_all(out, "exp", 0, 0, axis_index_groups=FAR, tiled=True)
-    mine = arrived.reshape(MEMBERS * CAP, width)
+    mine = arrived.reshape(MEMBERS * CAP, width + RIDER)
     theirs = lax.ppermute(mine, "exp", BESIDE)
+    part = jnp.sum(mine[:, width:], axis=0, dtype=f32) + jnp.sum(theirs[:, width:], axis=0, dtype=f32)
+    part = jnp.sum(part[: 3 * SLICE].reshape(3, SLICE), axis=0, keepdims=True)
+    part = part + lax.ppermute(part, "exp", TWIN)
+    mine, theirs = mine[:, :width], theirs[:, :width]
 
     def expert(rows):
         total = 0.0
@@ -81,16 +91,13 @@
 
     back = lax.ppermute(expert(theirs).astype(bf), "exp", BESIDE)
     both = (expert(mine) + back.astype(f32)).astype(bf).reshape(MEMBERS, CAP, width)
+    both = jnp.concatenate([both, riders(jnp.broadcast_to(part, (MEMBERS, SLICE)))], axis=2)
     returned = lax.all_to_all(both, "exp", 0, 0, axis_index_groups=FAR, tiled=True)
-    summed = jnp.sum(returned.reshape(EXPERTS, SPREAD, CAP, width), axis=1, dtype=f32)
+    mass = jnp.sum(returned[:, 0, width : width + 3 * SLICE].astype(f32).reshape(MEMBERS, 3, SLICE), axis=1).reshape(-1)
+    summed = jnp.sum(returned[:, :, :width].reshape(EXPERTS, SPREAD, CAP, width), axis=1, dtype=f32)
     scale = jnp.where(placed, gate[:, :, None], 0.0).reshape(tok_rows, EXPERTS * CAP)
     combined = jnp.dot(scale, summed.reshape(EXPERTS * CAP, width), precision=lax.Precision.HIGHEST)
     return combined.astype(bf), mass
-
-
-CG = [[place(c, r, k) for k in range(CORES)] for c in range(COLS) for r in range(RINGS)]
-XG = [[place(c, r, k) for c in range(COLS)] for r in range(RINGS) for k in range(CORES)]
-ZG = [[place(c, r, k) for r in range(RINGS)] for c in range(COLS) for k in range(CORES)]
 
 
 def solution(mesh):

time: 143 us -> 133 us (0.930)
  the two profiles are of different devices: /device:TPU:24 before, /device:TPU:57 now
where the time goes in v2:
time: 133 us; the launch traced here: 132 us
  waiting for transfers between devices  69.1 us (52%)
  starting transfers between devices  39 us (29%)
  matrix products  16 us (12%)
  other arithmetic  4.83 us (4%)
  local copies, waits for them, and re-layouts  1.9 us (1%)
    all_to_all x1, waiting for transfers between devices, shards(): lax.all_to_all(both, 'exp', 0, 0, axis_index_groups=FAR, tiled=True)  29.5 us
    all_to_all x1, waiting for transfers between devices, shards(): lax.all_to_all(out, 'exp', 0, 0, axis_index_groups=FAR, tiled=True)  21.8 us
    all_to_all x1, starting transfers between devices, shards(): lax.all_to_all(out, 'exp', 0, 0, axis_index_groups=FAR, tiled=True)  16.3 us
    ppermute x1, waiting for transfers between devices, shards(): back = lax.ppermute(expert(theirs).astype(bf), 'exp', BESIDE)  11.9 us
    dot_general x4, matrix products, expert(): total = total + jnp.dot(h, dw, preferred_element_type=f32)  8.55 us
    ppermute x3, starting transfers between devices, shards(): twins = tuple((lax.ppermute(w, 'exp', TWIN) for w in weights))  7.2 us
    all_to_all x1, starting transfers between devices, shards(): lax.all_to_all(both, 'exp', 0, 0, axis_index_groups=FAR, tiled=True)  6.85 us
    ppermute x1, waiting for transfers between devices, shards(): theirs = lax.ppermute(mine, 'exp', BESIDE)  5.86 us
  transfers between devices with their start and end apart: 8, of which 4 were waited for; matrix products, arithmetic and copies ran while one was open for 9% of the time, Pallas kernels for 0%

profile of v2, /device:TPU:57, one launch (start us, length us, event | category | flops | bytes accessed | tf_op | source)
XLA Modules:
  0.0 131.8 jit_solution(8947498382573974523)
XLA Ops:
  0.6 0.0 copy-start
  0.6 0.9 iota_compare_fusion
  1.6 0.0 copy-start.4
  1.6 2.3 %fusion.9 = f32[384]{0:T(512)S(1)} fusion(f32[32,8,1]{0,2,1:T(1,128)} %bitcast.59, s32[32,8]{0,1:T(8,128)} %param.7), kind=kOutput, calls=%fused_computation.16 | convolution fusion | flops 1376256 | bytes 3584 | tf_op jit(solution)/shard_map/tk,tke->e/dot_general | solution.py:61
  3.9 0.1 eq.45
  4.0 0.1 reshape.43
  4.1 0.1 maximum_bitcast_fusion
  4.2 0.1 fusion.8
  4.4 0.0 copy-done.4
  4.4 0.0 copy-done
  4.4 0.2 convolution_convert_fusion
  4.7 0.2 broadcast_in_dim.83
  5.0 0.0 copy-start.1
  5.0 0.0 copy-start.2
  5.0 1.2 fusion.16
  6.2 16.3 %all-to-all-start = ((bf16[32,2,3712]{2,1,0:T(2,128)(2,1)}), bf16[32,2,3712]{2,1,0:T(2,128)(2,1)S(1)}, u32[]{:S(2)}, u32[]{:S(2)}) async-start(bf16[32,2,3712]{2,1,0:T(2,128)(2,1)} %fusion.16), calls=%async_computation | async-start | bytes 950272 | tf_op jit(solution)/shard_map/all_to_all | solution.py:75
  22.5 0.0 copy-done.1
  22.5 2.9 %collective-permute-start.1 = (bf16[3584,128]{1,0:T(8,128)(2,1)S(1)}, bf16[3584,128]{1,0:T(8,128)(2,1)}, u32[]{:S(2)}, u32[]{:S(2)}) collective-permute-start(bf16[3584,128]{1,0:T(8,128)(2,1)S(1)} %copy-done.1), channel_id=1, source_target_pairs={{0,1},{1,0},{2,3},{3,2},{4,5},{5,4},{6,7},{7,6},{8,9},{9,8},{10,11... | collective-permute-start | bytes 2752520 | tf_op jit(solution)/shard_map/ppermute | solution.py:57
  25.4 0.0 copy-done.2
  25.4 1.9 %collective-permute-start = (bf16[3584,128]{1,0:T(8,128)(2,1)S(1)}, bf16[3584,128]{1,0:T(8,128)(2,1)}, u32[]{:S(2)}, u32[]{:S(2)}) collective-permute-start(bf16[3584,128]{1,0:T(8,128)(2,1)S(1)} %copy-done.2), channel_id=1, source_target_pairs={{0,1},{1,0},{2,3},{3,2},{4,5},{5,4},{6,7},{7,6},{8,9},{9,8},{10,11... | collective-permute-start | bytes 2752520 | tf_op jit(solution)/shard_map/ppermute | solution.py:57
  27.4 2.4 %collective-permute-start.2 = (bf16[128,3584]{1,0:T(8,128)(2,1)}, bf16[128,3584]{1,0:T(8,128)(2,1)}, u32[]{:S(2)}, u32[]{:S(2)}) collective-permute-start(bf16[128,3584]{1,0:T(8,128)(2,1)} %param.11), channel_id=1, source_target_pairs={{0,1},{1,0},{2,3},{3,2},{4,5},{5,4},{6,7},{7,6},{8,9},{9,8},{10,11... | collective-permute-start | bytes 2752520 | tf_op jit(solution)/shard_map/ppermute | solution.py:57
  29.8 21.8 %all-to-all-done = bf16[32,2,3712]{2,1,0:T(2,128)(2,1)S(1)} async-done(((bf16[32,2,3712]{2,1,0:T(2,128)(2,1)}), bf16[32,2,3712]{2,1,0:T(2,128)(2,1)S(1)}, u32[]{:S(2)}, u32[]{:S(2)}) %all-to-all-start) | async-done | bytes 475168 | tf_op jit(solution)/shard_map/all_to_all | solution.py:75
  51.6 0.2 reshape.44
  51.8 1.9 %collective-permute-start.3 = (bf16[64,3712]{1,0:T(8,128)(2,1)S(1)}, bf16[64,3712]{1,0:T(8,128)(2,1)S(1)}, u32[]{:S(2)}, u32[]{:S(2)}) collective-permute-start(bf16[64,3712]{1,0:T(8,128)(2,1)S(1)} %reshape.44), channel_id=1, source_target_pairs={{0,2},{1,3},{2,0},{3,1},{4,6},{5,7},{6,4},{7,5},{8,10},{9,11},{10,... | collective-permute-start | bytes 1425416 | tf_op jit(solution)/shard_map/ppermute | solution.py:77
  53.7 0.3 fusion.32
  54.0 0.0 collective-permute-done.1
  54.0 1.5 %fusion.26 = f32[64,128]{1,0:T(8,128)S(1)} fusion(bf16[3584,128]{1,0:T(8,128)(2,1)} %collective-permute-done.1, bf16[64,3712]{1,0:T(8,128)(2,1)S(1)} %reshape.44), kind=kOutput, calls=%fused_computation.33 | convolution fusion | flops 58720256 | bytes 1409024 | tf_op jit(solution)/shard_map/dot_general | solution.py:87
  55.6 2.7 %fusion.7 = f32[64,3584]{1,0:T(8,128)} fusion(bf16[128,3584]{1,0:T(8,128)(2,1)} %param.11, bf16[3584,128]{1,0:T(8,128)(2,1)S(1)} %copy-done.1, bf16[64,3712]{1,0:T(8,128)(2,1)S(1)} %reshape.44, f32[64,128]{1,0:T(8,128)S(1)} %fusion.32), kind=kOutput, calls=%fused_computation.13 | convolution fusion | flops 117489664 | bytes 3244032 | tf_op jit(solution)/shard_map/dot_general | solution.py:89
  58.2 5.9 %collective-permute-done.3 = bf16[64,3712]{1,0:T(8,128)(2,1)S(1)} collective-permute-done((bf16[64,3712]{1,0:T(8,128)(2,1)S(1)}, bf16[64,3712]{1,0:T(8,128)(2,1)S(1)}, u32[]{:S(2)}, u32[]{:S(2)}) %collective-permute-start.3) | collective-permute-done | bytes 475168 | tf_op jit(solution)/shard_map/ppermute | solution.py:77
  64.1 0.1 reshape.46
  64.2 4.8 %collective-permute-start.5 = (f32[1,12]{1,0:T(1,128)S(1)}, f32[1,12]{1,0:T(1,128)S(1)}, u32[]{:S(2)}, u32[]{:S(2)}) collective-permute-start(f32[1,12]{1,0:T(1,128)S(1)} %bitcast.60), channel_id=1, source_target_pairs={{0,1},{1,0},{2,3},{3,2},{4,5},{5,4},{6,7},{7,6},{8,9},{9,8},{10,11... | collective-permute-start | bytes 152 | tf_op jit(solution)/shard_map/ppermute | solution.py:80
  69.0 0.3 fusion.22
  69.3 1.5 %fusion.18 = f32[64,128]{1,0:T(8,128)S(1)} fusion(bf16[3584,128]{1,0:T(8,128)(2,1)} %collective-permute-done.1, bf16[64,3712]{1,0:T(8,128)(2,1)S(1)} %collective-permute-done.3), kind=kOutput, calls=%fused_computation.25 | convolution fusion | flops 58720256 | bytes 1409024 | tf_op jit(solution)/shard_map/dot_general | solution.py:87
  70.8 1.7 %fusion.44 = f32[64,3584]{1,0:T(8,128)S(1)} fusion(bf16[128,3584]{1,0:T(8,128)(2,1)} %param.11, f32[64,128]{1,0:T(8,128)S(1)} %fusion.22, bf16[3584,128]{1,0:T(8,128)(2,1)S(1)} %copy-done.2, bf16[64,3712]{1,0:T(8,128)(2,1)S(1)} %collective-permute-done.3), kind=kOutput, calls=%fused_computation.53 | convolution fusion | flops 117489664 | bytes 3244032 | tf_op jit(solution)/shard_map/dot_general | solution.py:89
  72.6 0.0 collective-permute-done
  72.6 0.0 copy-start.3
  72.6 0.0 collective-permute-done.2
  72.6 2.1 %fusion.2 = bf16[64,3584]{1,0:T(8,128)(2,1)S(1)} fusion(f32[64,3584]{1,0:T(8,128)S(1)} %fusion.44, bf16[128,3584]{1,0:T(8,128)(2,1)} %collective-permute-done.2, f32[64,128]{1,0:T(8,128)S(1)} %fusion.18, bf16[3584,128]{1,0:T(8,128)(2,1)} %collective-permute-done, bf16[64,3712]{1,0:T(8,128)(2,1)S(1)} %collective-permute-done.3), kind=kOutput, calls=%fused_computation.4 | convolution fusion | flops 117948416 | bytes 3702784 | tf_op jit(solution)/shard_map/dot_general | solution.py:89
  74.7 1.9 %collective-permute-start.4 = (bf16[64,3584]{1,0:T(8,128)(2,1)S(1)}, bf16[64,3584]{1,0:T(8,128)(2,1)S(1)}, u32[]{:S(2)}, u32[]{:S(2)}) collective-permute-start(bf16[64,3584]{1,0:T(8,128)(2,1)S(1)} %fusion.2), channel_id=1, source_target_pairs={{0,2},{1,3},{2,0},{3,1},{4,6},{5,7},{6,4},{7,5},{8,10},{9,11},{10,... | collective-permute-start | bytes 1376264 | tf_op jit(solution)/shard_map/ppermute | solution.py:92
  76.6 0.0 collective-permute-done.5
  76.7 0.1 maximum_maximum_fusion
  76.8 11.9 %collective-permute-done.4 = bf16[64,3584]{1,0:T(8,128)(2,1)S(1)} collective-permute-done((bf16[64,3584]{1,0:T(8,128)(2,1)S(1)}, bf16[64,3584]{1,0:T(8,128)(2,1)S(1)}, u32[]{:S(2)}, u32[]{:S(2)}) %collective-permute-start.4) | collective-permute-done | bytes 458784 | tf_op jit(solution)/shard_map/ppermute | solution.py:92
  88.7 0.0 copy-done.3
  88.7 2.0 %fusion.1 = bf16[64,3584]{1,0:T(8,128)(2,1)S(1)} fusion(f32[64,3584]{1,0:T(8,128)S(1)} %copy-done.3, bf16[128,3584]{1,0:T(8,128)(2,1)} %collective-permute-done.2, bf16[64,3584]{1,0:T(8,128)(2,1)S(1)} %collective-permute-done.4, f32[64,128]{1,0:T(8,128)S(1)} %fusion.26, bf16[3584,128]{1,0:T(8,128)(2,1)} %collective-permute-done, ...), kind=kOutput, calls=%fused_computation.3 | convolution fusion | flops 118407168 | bytes 4161536 | tf_op jit(solution)/shard_map/dot_general | solution.py:89
  90.7 0.2 reshape.45
  90.9 0.0 copy-start.5
  90.9 1.2 fusion.17
  92.1 6.9 %all-to-all-start.1 = ((bf16[32,2,3712]{2,1,0:T(2,128)(2,1)}), bf16[32,2,3712]{2,1,0:T(2,128)(2,1)S(1)}, u32[]{:S(2)}, u32[]{:S(2)}) async-start(bf16[32,2,3712]{2,1,0:T(2,128)(2,1)} %fusion.17), calls=%async_computation.1 | async-start | bytes 950272 | tf_op jit(solution)/shard_map/all_to_all | solution.py:95
  99.0 0.0 copy-done.5
  99.0 0.7 select_reduce_fusion
  99.7 29.5 %all-to-all-done.1 = bf16[32,2,3712]{2,1,0:T(2,128)(2,1)S(1)} async-done(((bf16[32,2,3712]{2,1,0:T(2,128)(2,1)}), bf16[32,2,3712]{2,1,0:T(2,128)(2,1)S(1)}, u32[]{:S(2)}, u32[]{:S(2)}) %all-to-all-start.1) | async-done | bytes 475168 | tf_op jit(solution)/shard_map/all_to_all | solution.py:95
  129.2 0.1 copy.43
  129.3 0.1 copy.44
  129.4 0.7 reshape.47
  130.1 0.4 convert_reduce_fusion
  130.5 1.3 fusion.3
  (21 shorter events, 0.3 us)
Async XLA Ops:
  0.6 3.8 %copy-start = (bf16[32,3584]{1,0:T(8,128)(2,1)S(1)}, bf16[32,3584]{1,0:T(8,128)(2,1)}, u32[]{:S(2)}) copy-start(bf16[32,3584]{1,0:T(8,128)(2,1)} %param.6) | copy-start | bytes 688132
  1.6 2.8 %copy-start.4 = (pred[32,8,384]{0,2,1:T(8,128)(4,1)}, pred[32,8,384]{0,2,1:T(8,128)(4,1)S(1)}, u32[]{:S(2)}) copy-start(pred[32,8,384]{0,2,1:T(8,128)(4,1)S(1)} %iota_compare_fusion) | copy-start | bytes 294916
  5.0 17.6 %copy-start.1 = (bf16[3584,128]{1,0:T(8,128)(2,1)S(1)}, bf16[3584,128]{1,0:T(8,128)(2,1)}, u32[]{:S(2)}) copy-start(bf16[3584,128]{1,0:T(8,128)(2,1)} %param.10) | copy-start | bytes 2752516
  5.0 20.4 %copy-start.2 = (bf16[3584,128]{1,0:T(8,128)(2,1)S(1)}, bf16[3584,128]{1,0:T(8,128)(2,1)}, u32[]{:S(2)}) copy-start(bf16[3584,128]{1,0:T(8,128)(2,1)} %param.9) | copy-start | bytes 2752516
  6.2 45.4 %all-to-all-start = ((bf16[32,2,3712]{2,1,0:T(2,128)(2,1)}), bf16[32,2,3712]{2,1,0:T(2,128)(2,1)S(1)}, u32[]{:S(2)}, u32[]{:S(2)}) async-start(bf16[32,2,3712]{2,1,0:T(2,128)(2,1)} %fusion.16), calls=%async_computation | async-start | bytes 950272 | tf_op jit(solution)/shard_map/all_to_all | solution.py:75
  22.5 31.5 %collective-permute-start.1 = (bf16[3584,128]{1,0:T(8,128)(2,1)S(1)}, bf16[3584,128]{1,0:T(8,128)(2,1)}, u32[]{:S(2)}, u32[]{:S(2)}) collective-permute-start(bf16[3584,128]{1,0:T(8,128)(2,1)S(1)} %copy-done.1), channel_id=1, source_target_pairs={{0,1},{1,0},{2,3},{3,2},{4,5},{5,4},{6,7},{7,6},{8,9},{9,8},{10,11... | collective-permute-start | bytes 2752520 | tf_op jit(solution)/shard_map/ppermute | solution.py:57
  25.4 47.1 %collective-permute-start = (bf16[3584,128]{1,0:T(8,128)(2,1)S(1)}, bf16[3584,128]{1,0:T(8,128)(2,1)}, u32[]{:S(2)}, u32[]{:S(2)}) collective-permute-start(bf16[3584,128]{1,0:T(8,128)(2,1)S(1)} %copy-done.2), channel_id=1, source_target_pairs={{0,1},{1,0},{2,3},{3,2},{4,5},{5,4},{6,7},{7,6},{8,9},{9,8},{10,11... | collective-permute-start | bytes 2752520 | tf_op jit(solution)/shard_map/ppermute | solution.py:57
  27.4 45.2 %collective-permute-start.2 = (bf16[128,3584]{1,0:T(8,128)(2,1)}, bf16[128,3584]{1,0:T(8,128)(2,1)}, u32[]{:S(2)}, u32[]{:S(2)}) collective-permute-start(bf16[128,3584]{1,0:T(8,128)(2,1)} %param.11), channel_id=1, source_target_pairs={{0,1},{1,0},{2,3},{3,2},{4,5},{5,4},{6,7},{7,6},{8,9},{9,8},{10,11... | collective-permute-start | bytes 2752520 | tf_op jit(solution)/shard_map/ppermute | solution.py:57
  51.8 12.3 %collective-permute-start.3 = (bf16[64,3712]{1,0:T(8,128)(2,1)S(1)}, bf16[64,3712]{1,0:T(8,128)(2,1)S(1)}, u32[]{:S(2)}, u32[]{:S(2)}) collective-permute-start(bf16[64,3712]{1,0:T(8,128)(2,1)S(1)} %reshape.44), channel_id=1, source_target_pairs={{0,2},{1,3},{2,0},{3,1},{4,6},{5,7},{6,4},{7,5},{8,10},{9,11},{10,... | collective-permute-start | bytes 1425416 | tf_op jit(solution)/shard_map/ppermute | solution.py:77
  64.2 12.4 %collective-permute-start.5 = (f32[1,12]{1,0:T(1,128)S(1)}, f32[1,12]{1,0:T(1,128)S(1)}, u32[]{:S(2)}, u32[]{:S(2)}) collective-permute-start(f32[1,12]{1,0:T(1,128)S(1)} %bitcast.60), channel_id=1, source_target_pairs={{0,1},{1,0},{2,3},{3,2},{4,5},{5,4},{6,7},{7,6},{8,9},{9,8},{10,11... | collective-permute-start | bytes 152 | tf_op jit(solution)/shard_map/ppermute | solution.py:80
  72.6 16.1 %copy-start.3 = (f32[64,3584]{1,0:T(8,128)S(1)}, f32[64,3584]{1,0:T(8,128)}, u32[]{:S(2)}) copy-start(f32[64,3584]{1,0:T(8,128)} %fusion.7) | copy-start | bytes 2752516
  74.7 14.0 %collective-permute-start.4 = (bf16[64,3584]{1,0:T(8,128)(2,1)S(1)}, bf16[64,3584]{1,0:T(8,128)(2,1)S(1)}, u32[]{:S(2)}, u32[]{:S(2)}) collective-permute-start(bf16[64,3584]{1,0:T(8,128)(2,1)S(1)} %fusion.2), channel_id=1, source_target_pairs={{0,2},{1,3},{2,0},{3,1},{4,6},{5,7},{6,4},{7,5},{8,10},{9,11},{10,... | collective-permute-start | bytes 1376264 | tf_op jit(solution)/shard_map/ppermute | solution.py:92
  90.9 8.1 %copy-start.5 = (f32[32,8]{0,1:T(8,128)S(1)}, f32[32,8]{0,1:T(8,128)}, u32[]{:S(2)}) copy-start(f32[32,8]{0,1:T(8,128)} %param.8) | copy-start | bytes 3076
  92.1 37.1 %all-to-all-start.1 = ((bf16[32,2,3712]{2,1,0:T(2,128)(2,1)}), bf16[32,2,3712]{2,1,0:T(2,128)(2,1)S(1)}, u32[]{:S(2)}, u32[]{:S(2)}) async-start(bf16[32,2,3712]{2,1,0:T(2,128)(2,1)} %fusion.17), calls=%async_computation.1 | async-start | bytes 950272 | tf_op jit(solution)/shard_map/all_to_all | solution.py:95

commit v3 on v1

v3 whole, which is shorter than its diff:
```python
import functools

import jax
import jax.numpy as jnp
from jax import lax
from jax.experimental import pallas as pl
from jax.experimental.pallas import tpu as pltpu
from jax.sharding import PartitionSpec as P

EXPERTS_ALL = 384
EXPERTS = 8
CAP = 2
COLS, RINGS, CORES = 4, 16, 2
PAIRS = RINGS // 2
CHUNKS = 1
F32, BF16, I32 = jnp.float32, jnp.bfloat16, jnp.int32


def place(col, ring, core):
    return (col * RINGS + ring) * CORES + core


def far_groups():
    groups = []
    for side in range(2):
        for core in range(CORES):
            members = []
            for col in range(COLS):
                for spot in range(PAIRS):
                    pair = (spot + 6 + 4 * side) % PAIRS
                    ring = 2 * pair + (side if pair < PAIRS // 2 else 1 - side)
                    members.append(place(col, ring, core))
            groups.append(members)
    return groups


FAR = far_groups()
MEMBERS = COLS * PAIRS
SPREAD = MEMBERS // EXPERTS
ROWS = MEMBERS * CAP
BESIDE = [(i, i ^ CORES) for i in range(COLS * RINGS * CORES)]
TWIN = [(i, i ^ 1) for i in range(COLS * RINGS * CORES)]
SLICE = EXPERTS_ALL // MEMBERS
RIDER = 128


def split3(v):
    a = v.astype(BF16)
    r = v - a.astype(F32)
    b = r.astype(BF16)
    c = (r - b.astype(F32)).astype(BF16)
    return a, b, c


def by_slice(e):
    return (e * 171) >> 11


def expert_of(member, side):
    spot = member & (PAIRS - 1)
    inner = (spot >= 2) & (spot < 6)
    return 2 * (member >> 3) + jnp.where(inner, side, 1 - side)


def slice_of(member, side):
    return (member & ~(PAIRS - 1)) + ((member + 6 + 4 * side) & (PAIRS - 1))


def iota(shape, axis):
    return lax.broadcasted_iota(I32, shape, axis)


def whole():
    return pl.BlockSpec(memory_space=pltpu.VMEM)


def scalar():
    return pl.BlockSpec(memory_space=pltpu.SMEM)


def pack_kernel(side_ref, tok_hbm, ids_ref, score_ref, out_ref, scale_ref, tok_ref, flip_ids, flip_score, sem):
    fetch = pltpu.make_async_copy(tok_hbm, tok_ref, sem)
    fetch.start()
    side = side_ref[0]
    rows, width = tok_ref.shape
    top = ids_ref.shape[0]
    flip_ids[...] = jnp.zeros_like(flip_ids)
    flip_score[...] = jnp.zeros_like(flip_score)
    flip_ids[:top, :rows] = ids_ref[...]
    flip_score[:top, :rows] = score_ref[...]
    ids, score = flip_ids[...].T[:rows], flip_score[...].T[:rows]
    every = iota((rows, EXPERTS_ALL), 1)
    column = iota((rows, 128), 1)
    named = jnp.where(column < ROWS, expert_of(column >> 1, side), -1)
    mass = jnp.zeros((rows, EXPERTS_ALL), F32)
    gate = jnp.zeros((rows, 128), F32)
    hit = jnp.zeros((rows, 128), F32)
    for k in range(top):
        one, s = ids[:, k : k + 1], score[:, k : k + 1]
        mass = mass + jnp.where(every == one, s, 0.0)
        same = named == one
        gate = gate + jnp.where(same, s, 0.0)
        hit = hit + jnp.where(same, 1.0, 0.0)
    lower = jnp.where(iota((rows, rows), 0) >= iota((rows, rows), 1), 1.0, 0.0)
    rank = jnp.dot(lower.astype(BF16), hit.astype(BF16), preferred_element_type=F32) - 1.0
    slot = (column & 1).astype(F32)
    placed = (hit > 0.5) & (rank == slot)
    scale = split3(jnp.where(placed, gate, 0.0))
    for i, part in enumerate(scale):
        scale_ref[i * rows : (i + 1) * rows, :] = part
    pick = jnp.where(placed, 1.0, 0.0).T[:ROWS].astype(BF16)
    fetch.wait()
    out_ref[:, :width] = jnp.dot(pick, tok_ref[...], preferred_element_type=F32).astype(BF16)
    load = jnp.sum(mass, axis=0, keepdims=True)
    row, e = iota((ROWS, EXPERTS_ALL), 0), iota((ROWS, EXPERTS_ALL), 1)
    mine = ((row & 1) == 0) & (slice_of(row >> 1, side) == by_slice(e))
    e2, lane = iota((EXPERTS_ALL, RIDER), 0), iota((EXPERTS_ALL, RIDER), 1)
    within = e2 - SLICE * by_slice(e2)
    rider = jnp.zeros((ROWS, RIDER), F32)
    for i, term in enumerate(split3(load)):
        spread = jnp.where(mine, term.astype(F32), 0.0).astype(BF16)
        select = jnp.where(lane == within + i * SLICE, 1.0, 0.0).astype(BF16)
        rider = rider + jnp.dot(spread, select, preferred_element_type=F32)
    out_ref[:, width:] = rider.astype(BF16)


def pack(side, tokens, ids, scores):
    rows, width = tokens.shape
    return pl.pallas_call(
        pack_kernel,
        out_shape=(
            jax.ShapeDtypeStruct((ROWS, width + RIDER), BF16),
            jax.ShapeDtypeStruct((3 * rows, 128), BF16),
        ),
        in_specs=[scalar(), pl.BlockSpec(memory_space=pl.ANY), whole(), whole()],
        out_specs=(whole(), whole()),
        scratch_shapes=[
            pltpu.VMEM((rows, width), BF16),
            pltpu.VMEM((128, 128), I32),
            pltpu.VMEM((128, 128), F32),
            pltpu.SemaphoreType.DMA(()),
        ],
        compiler_params=pltpu.CompilerParams(vmem_limit_bytes=6 << 20),
        name="pack",
    )(side, tokens, ids.T, scores.T)


def expert_kernel(x_ref, *refs):
    hbm, (out_ref, wide, down, sems) = refs[:6], refs[6:]
    width, hid = hbm[0].shape
    targets = [wide.at[i] for i in range(4)] + [down.at[pl.ds(i * hid, hid), :] for i in range(2)]
    copies = [pltpu.make_async_copy(ref, buf, sems.at[i]) for i, (ref, buf) in enumerate(zip(hbm, targets))]
    for copy in copies:
        copy.start()
    x = x_ref[:, :width]
    act = []
    for i in range(4):
        copies[i].wait()
        act.append(jnp.dot(x, wide[i], preferred_element_type=F32))
    g = jnp.concatenate(act[:2], axis=1)
    u = jnp.concatenate(act[2:], axis=1)
    h = (g / (1.0 + jnp.exp(-g)) * u).astype(BF16)
    copies[4].wait()
    copies[5].wait()
    out_ref[...] = jnp.dot(h, down[...], preferred_element_type=F32).astype(out_ref.dtype)


def expert(x, weights, twins, dtype):
    rows = x.shape[0]
    width, hid = weights[0].shape
    operands = [w for pair in zip(weights, twins) for w in pair]
    return pl.pallas_call(
        expert_kernel,
        out_shape=jax.ShapeDtypeStruct((rows, width), dtype),
        in_specs=[whole()] + [pl.BlockSpec(memory_space=pl.ANY)] * 6,
        out_specs=whole(),
        scratch_shapes=[
            pltpu.VMEM((4, width, hid), BF16),
            pltpu.VMEM((2 * hid, width), BF16),
            pltpu.SemaphoreType.DMA((6,)),
        ],
        cost_estimate=pl.CostEstimate(
            flops=12 * rows * width * hid, bytes_accessed=12 * width * hid, transcendentals=rows * 2 * hid
        ),
        compiler_params=pltpu.CompilerParams(vmem_limit_bytes=12 << 20),
        name="expert",
    )(x, *operands)


def join_kernel(own_ref, rider_ref, *refs):
    backs, out_ref = refs[:-1], refs[-1]
    width = own_ref.shape[1]
    first = 0
    for back in backs:
        span = pl.ds(first, back.shape[0])
        out_ref[span, :width] = (own_ref[span, :] + back[...].astype(F32)).astype(BF16)
        first += back.shape[0]
    even = (iota((ROWS, RIDER), 0) & 1) == 0
    out_ref[:, width:] = jnp.where(even, rider_ref[...], 0.0).astype(BF16)


def join(own, rider, backs):
    return pl.pallas_call(
        join_kernel,
        out_shape=jax.ShapeDtypeStruct((ROWS, own.shape[1] + RIDER), BF16),
        in_specs=[whole()] * (2 + len(backs)),
        out_specs=whole(),
        compiler_params=pltpu.CompilerParams(vmem_limit_bytes=6 << 20),
        name="join",
    )(own, rider, *backs)


def combine_kernel(side_ref, rows_ref, scale_ref, out_ref, mass_ref):
    side = side_ref[0]
    tok, width = out_ref.shape
    weight = scale_ref[:, :ROWS]
    parts = jnp.dot(weight, rows_ref[:, :width], preferred_element_type=F32)
    out_ref[...] = (parts[:tok] + parts[tok : 2 * tok] + parts[2 * tok :]).astype(BF16)
    lane, e = iota((RIDER, EXPERTS_ALL), 0), iota((RIDER, EXPERTS_ALL), 1)
    within = e - SLICE * by_slice(e)
    same = (lane == within) | (lane == within + SLICE) | (lane == within + 2 * SLICE)
    total = jnp.dot(rows_ref[:, width:], jnp.where(same, 1.0, 0.0).astype(BF16), preferred_element_type=F32)
    row, e2 = iota((ROWS, EXPERTS_ALL), 0), iota((ROWS, EXPERTS_ALL), 1)
    mine = ((row & 1) == 0) & (slice_of(row >> 1, side) == by_slice(e2))
    mass_ref[...] = jnp.sum(jnp.where(mine, total, 0.0), axis=0)


def combine(side, rows, scale, tok):
    width = rows.shape[1] - RIDER
    return pl.pallas_call(
        combine_kernel,
        out_shape=(jax.ShapeDtypeStruct((tok, width), BF16), jax.ShapeDtypeStruct((EXPERTS_ALL,), F32)),
        in_specs=[scalar(), whole(), whole()],
        out_specs=(whole(), whole()),
        compiler_params=pltpu.CompilerParams(vmem_limit_bytes=6 << 20),
        name="combine",
    )(side, rows, scale)


def far(rows):
    blocks = rows.reshape(MEMBERS, CAP, rows.shape[1])
    return lax.all_to_all(blocks, "exp", 0, 0, axis_index_groups=FAR, tiled=True).reshape(rows.shape)


def shards(tokens, expert_ids, gate_scores, gate_weight, up_weight, down_weight):
    tok_rows, width = tokens.shape
    weights = (gate_weight, up_weight, down_weight)
    twins = tuple(lax.ppermute(w, "exp", TWIN) for w in weights)
    ring = (lax.axis_index("exp") // CORES) % RINGS
    side = ((ring & 1) ^ (ring >> 3)).astype(I32).reshape(1)
    out, scale = pack(side, tokens, expert_ids, gate_scores)
    mine = far(out)
    step = ROWS // CHUNKS
    theirs = [lax.ppermute(mine[i * step : (i + 1) * step], "exp", BESIDE) for i in range(CHUNKS)]
    own = expert(mine, weights, twins, F32)
    partials = [expert(x, weights, twins, BF16) for x in theirs]
    backs = [lax.ppermute(p, "exp", BESIDE) for p in partials]
    part = sum(jnp.sum(x[:, width:], axis=0, dtype=F32) for x in [mine] + theirs)
    part = jnp.sum(part[: 3 * SLICE].reshape(3, SLICE), axis=0, keepdims=True)
    part, _ = lax.optimization_barrier((part, partials[-1]))
    part = part + lax.ppermute(part, "exp", TWIN)
    rider = jnp.concatenate([t.astype(F32) for t in split3(part)], axis=1)
    rider = jnp.pad(rider, ((0, 0), (0, RIDER - 3 * SLICE)))
    returned = far(join(own, rider, backs))
    combined, mass = combine(side, returned, scale, tok_rows)
    return combined, mass


def solution(mesh):
    return jax.shard_map(
        shards,
        mesh=mesh,
        in_specs=(
            P(("rep", "exp"), None),
            P(("rep", "exp"), None),
            P(("rep", "exp"), None),
            P(None, "exp"),
            P(None, "exp"),
            P("exp", None),
        ),
        out_specs=(P(("rep", "exp"), None), P("rep")),
        check_vma=False,
    )
```

time: 143 us -> 121 us (0.85)
  matrix products: 13.9 us -> 0 us
  Pallas kernels: 0 us -> 9.49 us
  starting transfers between devices: 41.7 us -> 32.6 us
  blocking collectives: 44.9 us -> 37.2 us
  local copies, waits for them, and re-layouts: 3.05 us -> 6.38 us
  waiting for transfers between devices: 35.4 us -> 32.7 us
  other arithmetic: 2.1 us -> 0.16 us
    psum x3 -> x0, blocking collectives: 44.9 us -> none  [the longest x1 31.7 us: shards(): lax.psum(lax.psum(lax.psum(mass, 'exp', axis_index_groups=CG), 'exp', axi...]
    all_to_all x0 -> x1, blocking collectives: none -> 37.2 us  [far(): lax.all_to_all(blocks, 'exp', 0, 0, axis_index_groups=FAR, tiled=True)]
    dot_general x12 -> x0, matrix products: 13.9 us -> none  [the longest x4 7.14 us: expert(): total = total + jnp.dot(h, dw, preferred_element_type=f32)]
    pallas_call x0 -> x5, Pallas kernels: none -> 9.49 us  [the longest x2 6.25 us: expert(): pl.pallas_call(expert_kernel, out_shape=jax.ShapeDtypeStruct((rows, width...]
    all_to_all x2 -> x1, starting transfers between devices: 25.6 us -> 18 us  [far(): lax.all_to_all(blocks, 'exp', 0, 0, axis_index_groups=FAR, tiled=True)]
    all_to_all x2 -> x1, waiting for transfers between devices: 24.4 us -> 18.6 us  [far(): lax.all_to_all(blocks, 'exp', 0, 0, axis_index_groups=FAR, tiled=True)]
    ppermute x2 -> x3, waiting for transfers between devices: 11 us -> 14 us  [the longest x1 10.4 us: shards(): lax.ppermute(mine[i * step:(i + 1) * step], 'exp', BESIDE)]
    unnamed x14 -> x16, local copies, waits for them, and re-layouts: 0.77 us -> 3.75 us
  transfers between devices with their start and end apart: 7 -> 7, of which waited for: 3 -> 4; matrix products, arithmetic and copies ran while one was open for 6% -> 1% of each run, Pallas kernels for 0% -> 2%
where the time goes in v3:
time: 121 us; the launch traced here: 119 us
  blocking collectives  37.2 us (31%)
  waiting for transfers between devices  32.7 us (27%)
  starting transfers between devices  32.6 us (27%)
  Pallas kernels  9.49 us (8%)
  local copies, waits for them, and re-layouts  6.38 us (5%)
    all_to_all x1, blocking collectives, far(): lax.all_to_all(blocks, 'exp', 0, 0, axis_index_groups=FAR, tiled=True)  37.2 us
    all_to_all x1, waiting for transfers between devices, far(): lax.all_to_all(blocks, 'exp', 0, 0, axis_index_groups=FAR, tiled=True)  18.6 us
    all_to_all x1, starting transfers between devices, far(): lax.all_to_all(blocks, 'exp', 0, 0, axis_index_groups=FAR, tiled=True)  18 us
    ppermute x1, waiting for transfers between devices, shards(): lax.ppermute(mine[i * step:(i + 1) * step], 'exp', BESIDE)  10.4 us
    pallas_call x2, Pallas kernels, expert(): pl.pallas_call(expert_kernel, out_shape=jax.ShapeDtypeStruct((rows, width...  6.25 us
    ppermute x3, starting transfers between devices, shards(): twins = tuple((lax.ppermute(w, 'exp', TWIN) for w in weights))  6.25 us
    unnamed x16, local copies, waits for them, and re-layouts  3.75 us
    ppermute x1, starting transfers between devices, shards(): backs = [lax.ppermute(p, 'exp', BESIDE) for p in partials]  3.65 us
  transfers between devices with their start and end apart: 7, of which 4 were waited for; matrix products, arithmetic and copies ran while one was open for 1% of the time, Pallas kernels for 2%

profile of v3, /device:TPU:24, one launch (start us, length us, event | category | flops | bytes accessed | tf_op | source)
XLA Modules:
  0.0 119.4 jit_solution(8907776227391298372)
XLA Ops:
  0.7 0.0 copy-start.7
  0.7 0.0 copy-start.6
  0.7 0.7 copy-done.7
  1.3 0.0 copy-done.6
  1.4 0.0 copy-start.5
  1.4 0.9 copy-done.5
  2.3 1.1 pack.1
  3.4 0.0 copy-start
  3.4 0.0 copy-start.1
  3.4 1.0 reshape.23
  4.4 0.0 copy-start.2
  4.4 18.0 %all-to-all-start = ((bf16[32,2,3712]{2,1,0:T(2,128)(2,1)}), bf16[32,2,3712]{2,1,0:T(2,128)(2,1)}, u32[]{:S(2)}, u32[]{:S(2)}) async-start(bf16[32,2,3712]{2,1,0:T(2,128)(2,1)} %reshape.23), calls=%async_computation | async-start | bytes 950272 | tf_op jit(solution)/shard_map/all_to_all | solution.py:242
  22.4 0.0 copy-done
  22.4 1.9 %collective-permute-start = (bf16[3584,128]{1,0:T(8,128)(2,1)S(1)}, bf16[3584,128]{1,0:T(8,128)(2,1)}, u32[]{:S(2)}, u32[]{:S(2)}) collective-permute-start(bf16[3584,128]{1,0:T(8,128)(2,1)S(1)} %copy-done), channel_id=1, source_target_pairs={{0,1},{1,0},{2,3},{3,2},{4,5},{5,4},{6,7},{7,6},{8,9},{9,8},{10,11... | collective-permute-start | bytes 2752520 | tf_op jit(solution)/shard_map/ppermute | solution.py:248
  24.3 0.0 copy-done.1
  24.3 2.4 %collective-permute-start.1 = (bf16[3584,128]{1,0:T(8,128)(2,1)S(1)}, bf16[3584,128]{1,0:T(8,128)(2,1)}, u32[]{:S(2)}, u32[]{:S(2)}) collective-permute-start(bf16[3584,128]{1,0:T(8,128)(2,1)S(1)} %copy-done.1), channel_id=1, source_target_pairs={{0,1},{1,0},{2,3},{3,2},{4,5},{5,4},{6,7},{7,6},{8,9},{9,8},{10,11... | collective-permute-start | bytes 2752520 | tf_op jit(solution)/shard_map/ppermute | solution.py:248
  26.8 1.9 %collective-permute-start.2 = (bf16[128,3584]{1,0:T(8,128)(2,1)}, bf16[128,3584]{1,0:T(8,128)(2,1)}, u32[]{:S(2)}, u32[]{:S(2)}) collective-permute-start(bf16[128,3584]{1,0:T(8,128)(2,1)} %refs_4_.3), channel_id=1, source_target_pairs={{0,1},{1,0},{2,3},{3,2},{4,5},{5,4},{6,7},{7,6},{8,9},{9,8},{10,11... | collective-permute-start | bytes 2752520 | tf_op jit(solution)/shard_map/ppermute | solution.py:248
  28.7 18.6 %all-to-all-done = bf16[32,2,3712]{2,1,0:T(2,128)(2,1)} async-done(((bf16[32,2,3712]{2,1,0:T(2,128)(2,1)}), bf16[32,2,3712]{2,1,0:T(2,128)(2,1)}, u32[]{:S(2)}, u32[]{:S(2)}) %all-to-all-start) | async-done | bytes 475168 | tf_op jit(solution)/shard_map/all_to_all | solution.py:242
  47.3 1.2 %reshape.24.x_ref = bf16[64,3712]{1,0:T(8,128)(2,1)S(1)} reshape(bf16[32,2,3712]{2,1,0:T(2,128)(2,1)} %all-to-all-done) | data formatting | bytes 950272 | tf_op jit(solution)/shard_map/reshape | solution.py:242
  48.5 2.8 %collective-permute-start.3 = (bf16[64,3712]{1,0:T(8,128)(2,1)S(1)}, bf16[64,3712]{1,0:T(8,128)(2,1)S(1)}, u32[]{:S(2)}, u32[]{:S(2)}) collective-permute-start(bf16[64,3712]{1,0:T(8,128)(2,1)S(1)} %reshape.24.x_ref), channel_id=1, source_target_pairs={{0,2},{1,3},{2,0},{3,1},{4,6},{5,7},{6,4},{7,5},{8,10},{9,11},{10,... | collective-permute-start | bytes 1425416 | tf_op jit(solution)/shard_map/ppermute | solution.py:254
  51.3 0.0 collective-permute-done.refs_1_
  51.3 0.0 collective-permute-done.1.refs_3_
  51.3 0.0 collective-permute-done.2.refs_5_
  51.4 10.4 %collective-permute-done.3.x_ref = bf16[64,3712]{1,0:T(8,128)(2,1)S(1)} collective-permute-done((bf16[64,3712]{1,0:T(8,128)(2,1)S(1)}, bf16[64,3712]{1,0:T(8,128)(2,1)S(1)}, u32[]{:S(2)}, u32[]{:S(2)}) %collective-permute-start.3) | collective-permute-done | bytes 475168 | tf_op jit(solution)/shard_map/ppermute | solution.py:254
  61.7 0.0 copy-done.2
  61.7 3.5 %expert.3 = bf16[64,3584]{1,0:T(8,128)(2,1)} custom-call(bf16[64,3712]{1,0:T(8,128)(2,1)S(1)} %collective-permute-done.3.x_ref, bf16[3584,128]{1,0:T(8,128)(2,1)S(1)} %copy-done, bf16[3584,128]{1,0:T(8,128)(2,1)} %collective-permute-done.refs_1_, bf16[3584,128]{1,0:T(8,128)(2,1)S(1)} %copy-done.1, bf16[3584,128]{1,0:T(8,128)(2,1)} %collective-permute-done.1.refs_3_, ...), custom_call_target="tpu_custom_call" | custom-call | flops 352321536 | bytes 5505024 | tf_op jit(solution)/shard_map/expert/pallas_call | solution.py:172
  65.2 3.6 %collective-permute-start.5 = (bf16[64,3584]{1,0:T(8,128)(2,1)}, bf16[64,3584]{1,0:T(8,128)(2,1)}, u32[]{:S(2)}, u32[]{:S(2)}) collective-permute-start(bf16[64,3584]{1,0:T(8,128)(2,1)} %expert.3), channel_id=1, source_target_pairs={{0,2},{1,3},{2,0},{3,1},{4,6},{5,7},{6,4},{7,5},{8,10},{9,11},{10,... | collective-permute-start | bytes 1376264 | tf_op jit(solution)/shard_map/ppermute | solution.py:257
  68.9 2.7 %expert.2.own_ref = f32[64,3584]{1,0:T(8,128)S(1)} custom-call(bf16[64,3712]{1,0:T(8,128)(2,1)S(1)} %reshape.24.x_ref, bf16[3584,128]{1,0:T(8,128)(2,1)S(1)} %copy-done, bf16[3584,128]{1,0:T(8,128)(2,1)} %collective-permute-done.refs_1_, bf16[3584,128]{1,0:T(8,128)(2,1)S(1)} %copy-done.1, bf16[3584,128]{1,0:T(8,128)(2,1)} %collective-permute-done.1.refs_3_, ...), custom_call_target="tpu_custom_call" | custom-call | flops 352321536 | bytes 5505024 | tf_op jit(solution)/shard_map/expert/pallas_call | solution.py:172
  71.6 0.0 copy-start.3
  71.6 0.9 copy-done.3
  72.6 0.1 reshape.25
  72.7 1.9 %collective-permute-start.4 = (f32[1,12]{1,0:T(1,128)S(1)}, f32[1,12]{1,0:T(1,128)S(1)}, u32[]{:S(2)}, u32[]{:S(2)}) collective-permute-start(f32[1,12]{1,0:T(1,128)S(1)} %bitcast.7), channel_id=1, source_target_pairs={{0,1},{1,0},{2,3},{3,2},{4,5},{5,4},{6,7},{7,6},{8,9},{9,8},{10,11... | collective-permute-start | bytes 152 | tf_op jit(solution)/shard_map/ppermute | solution.py:261
  74.6 1.1 collective-permute-done.4
  75.8 0.1 select_maximum_fusion.rider_ref
  75.8 2.5 %collective-permute-done.5.refs_0_ = bf16[64,3584]{1,0:T(8,128)(2,1)} collective-permute-done((bf16[64,3584]{1,0:T(8,128)(2,1)}, bf16[64,3584]{1,0:T(8,128)(2,1)}, u32[]{:S(2)}, u32[]{:S(2)}) %collective-permute-start.5) | collective-permute-done | bytes 458784 | tf_op jit(solution)/shard_map/ppermute | solution.py:257
  78.4 0.0 copy-start.4
  78.4 1.2 copy-done.4
  79.6 1.1 join.1
  80.7 0.2 reshape.26
  80.9 37.2 %all_to_all.10 = bf16[32,2,3712]{2,1,0:T(2,128)(2,1)S(1)} all-to-all(bf16[32,2,3712]{2,1,0:T(2,128)(2,1)S(1)} %reshape.26), channel_id=1, replica_groups={{26,30,0,4,8,12,18,22,58,62,32,36,40,44,50,54,90,94,64,68,72,76,82,86,1..., dimensions={0} | all-to-all | bytes 950272 | tf_op jit(solution)/shard_map/all_to_all | solution.py:242
  118.1 0.2 reshape.27.rows_ref
  118.3 1.1 combine.1
  (5 shorter events, 0.1 us)
Async XLA Ops:
  0.7 0.7 copy-start.7
  0.7 0.7 copy-start.6
  1.4 0.9 copy-start.5
  3.4 19.0 %copy-start = (bf16[3584,128]{1,0:T(8,128)(2,1)S(1)}, bf16[3584,128]{1,0:T(8,128)(2,1)}, u32[]{:S(2)}) copy-start(bf16[3584,128]{1,0:T(8,128)(2,1)} %refs_0_.3) | copy-start | bytes 2752516
  3.4 20.9 %copy-start.1 = (bf16[3584,128]{1,0:T(8,128)(2,1)S(1)}, bf16[3584,128]{1,0:T(8,128)(2,1)}, u32[]{:S(2)}) copy-start(bf16[3584,128]{1,0:T(8,128)(2,1)} %refs_2_.3) | copy-start | bytes 2752516
  4.4 57.3 %copy-start.2 = (bf16[128,3584]{1,0:T(8,128)(2,1)S(1)}, bf16[128,3584]{1,0:T(8,128)(2,1)}, u32[]{:S(2)}) copy-start(bf16[128,3584]{1,0:T(8,128)(2,1)} %refs_4_.3) | copy-start | bytes 2752516
  4.4 42.9 %all-to-all-start = ((bf16[32,2,3712]{2,1,0:T(2,128)(2,1)}), bf16[32,2,3712]{2,1,0:T(2,128)(2,1)}, u32[]{:S(2)}, u32[]{:S(2)}) async-start(bf16[32,2,3712]{2,1,0:T(2,128)(2,1)} %reshape.23), calls=%async_computation | async-start | bytes 950272 | tf_op jit(solution)/shard_map/all_to_all | solution.py:242
  22.4 28.9 %collective-permute-start = (bf16[3584,128]{1,0:T(8,128)(2,1)S(1)}, bf16[3584,128]{1,0:T(8,128)(2,1)}, u32[]{:S(2)}, u32[]{:S(2)}) collective-permute-start(bf16[3584,128]{1,0:T(8,128)(2,1)S(1)} %copy-done), channel_id=1, source_target_pairs={{0,1},{1,0},{2,3},{3,2},{4,5},{5,4},{6,7},{7,6},{8,9},{9,8},{10,11... | collective-permute-start | bytes 2752520 | tf_op jit(solution)/shard_map/ppermute | solution.py:248
  24.3 27.0 %collective-permute-start.1 = (bf16[3584,128]{1,0:T(8,128)(2,1)S(1)}, bf16[3584,128]{1,0:T(8,128)(2,1)}, u32[]{:S(2)}, u32[]{:S(2)}) collective-permute-start(bf16[3584,128]{1,0:T(8,128)(2,1)S(1)} %copy-done.1), channel_id=1, source_target_pairs={{0,1},{1,0},{2,3},{3,2},{4,5},{5,4},{6,7},{7,6},{8,9},{9,8},{10,11... | collective-permute-start | bytes 2752520 | tf_op jit(solution)/shard_map/ppermute | solution.py:248
  26.8 24.6 %collective-permute-start.2 = (bf16[128,3584]{1,0:T(8,128)(2,1)}, bf16[128,3584]{1,0:T(8,128)(2,1)}, u32[]{:S(2)}, u32[]{:S(2)}) collective-permute-start(bf16[128,3584]{1,0:T(8,128)(2,1)} %refs_4_.3), channel_id=1, source_target_pairs={{0,1},{1,0},{2,3},{3,2},{4,5},{5,4},{6,7},{7,6},{8,9},{9,8},{10,11... | collective-permute-start | bytes 2752520 | tf_op jit(solution)/shard_map/ppermute | solution.py:248
  48.5 13.2 %collective-permute-start.3 = (bf16[64,3712]{1,0:T(8,128)(2,1)S(1)}, bf16[64,3712]{1,0:T(8,128)(2,1)S(1)}, u32[]{:S(2)}, u32[]{:S(2)}) collective-permute-start(bf16[64,3712]{1,0:T(8,128)(2,1)S(1)} %reshape.24.x_ref), channel_id=1, source_target_pairs={{0,2},{1,3},{2,0},{3,1},{4,6},{5,7},{6,4},{7,5},{8,10},{9,11},{10,... | collective-permute-start | bytes 1425416 | tf_op jit(solution)/shard_map/ppermute | solution.py:254
  65.2 13.2 %collective-permute-start.5 = (bf16[64,3584]{1,0:T(8,128)(2,1)}, bf16[64,3584]{1,0:T(8,128)(2,1)}, u32[]{:S(2)}, u32[]{:S(2)}) collective-permute-start(bf16[64,3584]{1,0:T(8,128)(2,1)} %expert.3), channel_id=1, source_target_pairs={{0,2},{1,3},{2,0},{3,1},{4,6},{5,7},{6,4},{7,5},{8,10},{9,11},{10,... | collective-permute-start | bytes 1376264 | tf_op jit(solution)/shard_map/ppermute | solution.py:257
  71.6 0.9 copy-start.3
  72.7 3.0 %collective-permute-start.4 = (f32[1,12]{1,0:T(1,128)S(1)}, f32[1,12]{1,0:T(1,128)S(1)}, u32[]{:S(2)}, u32[]{:S(2)}) collective-permute-start(f32[1,12]{1,0:T(1,128)S(1)} %bitcast.7), channel_id=1, source_target_pairs={{0,1},{1,0},{2,3},{3,2},{4,5},{5,4},{6,7},{7,6},{8,9},{9,8},{10,11... | collective-permute-start | bytes 152 | tf_op jit(solution)/shard_map/ppermute | solution.py:261
  78.4 1.2 copy-start.4

commit v4 on v3

--- a/solution.py
+++ b/solution.py
@@ -12,7 +12,7 @@
 CAP = 2
 COLS, RINGS, CORES = 4, 16, 2
 PAIRS = RINGS // 2
-CHUNKS = 1
+CHUNKS = 2
 F32, BF16, I32 = jnp.float32, jnp.bfloat16, jnp.int32
 
 
@@ -42,6 +42,7 @@
 TWIN = [(i, i ^ 1) for i in range(COLS * RINGS * CORES)]
 SLICE = EXPERTS_ALL // MEMBERS
 RIDER = 128
+TERMS = 3 * SLICE
 
 
 def split3(v):
@@ -110,7 +111,8 @@
         scale_ref[i * rows : (i + 1) * rows, :] = part
     pick = jnp.where(placed, 1.0, 0.0).T[:ROWS].astype(BF16)
     fetch.wait()
-    out_ref[:, :width] = jnp.dot(pick, tok_ref[...], preferred_element_type=F32).astype(BF16)
+    picked = jnp.dot(pick, tok_ref[...], preferred_element_type=F32).astype(BF16)
+    out_ref[:, :, :width] = picked.reshape(MEMBERS, CAP, width)
     load = jnp.sum(mass, axis=0, keepdims=True)
     row, e = iota((ROWS, EXPERTS_ALL), 0), iota((ROWS, EXPERTS_ALL), 1)
     mine = ((row & 1) == 0) & (slice_of(row >> 1, side) == by_slice(e))
@@ -121,7 +123,7 @@
         spread = jnp.where(mine, term.astype(F32), 0.0).astype(BF16)
         select = jnp.where(lane == within + i * SLICE, 1.0, 0.0).astype(BF16)
         rider = rider + jnp.dot(spread, select, preferred_element_type=F32)
-    out_ref[:, width:] = rider.astype(BF16)
+    out_ref[:, :, width:] = rider.astype(BF16).reshape(MEMBERS, CAP, RIDER)
 
 
 def pack(side, tokens, ids, scores):
@@ -129,7 +131,7 @@
     return pl.pallas_call(
         pack_kernel,
         out_shape=(
-            jax.ShapeDtypeStruct((ROWS, width + RIDER), BF16),
+            jax.ShapeDtypeStruct((MEMBERS, CAP, width + RIDER), BF16),
             jax.ShapeDtypeStruct((3 * rows, 128), BF16),
         ),
         in_specs=[scalar(), pl.BlockSpec(memory_space=pl.ANY), whole(), whole()],
@@ -145,14 +147,19 @@
     )(side, tokens, ids.T, scores.T)
 
 
-def expert_kernel(x_ref, *refs):
-    hbm, (out_ref, wide, down, sems) = refs[:6], refs[6:]
+def expert_kernel(n_sums, x_ref, *refs):
+    sums, hbm, (out_ref, sum_ref, wide, down, sems) = refs[:n_sums], refs[n_sums : n_sums + 6], refs[n_sums + 6 :]
     width, hid = hbm[0].shape
     targets = [wide.at[i] for i in range(4)] + [down.at[pl.ds(i * hid, hid), :] for i in range(2)]
     copies = [pltpu.make_async_copy(ref, buf, sems.at[i]) for i, (ref, buf) in enumerate(zip(hbm, targets))]
     for copy in copies:
         copy.start()
-    x = x_ref[:, :width]
+    rows = x_ref[...].reshape(-1, x_ref.shape[-1])
+    x = rows[:, :width]
+    total = jnp.sum(rows[:, width:].astype(F32), axis=0, keepdims=True)
+    for other in sums:
+        total = total + other[...]
+    sum_ref[...] = total
     act = []
     for i in range(4):
         copies[i].wait()
@@ -165,68 +172,76 @@
     out_ref[...] = jnp.dot(h, down[...], preferred_element_type=F32).astype(out_ref.dtype)
 
 
-def expert(x, weights, twins, dtype):
-    rows = x.shape[0]
+def expert(x, sums, weights, twins, dtype):
+    rows = x.shape[0] * CAP
     width, hid = weights[0].shape
     operands = [w for pair in zip(weights, twins) for w in pair]
     return pl.pallas_call(
-        expert_kernel,
-        out_shape=jax.ShapeDtypeStruct((rows, width), dtype),
-        in_specs=[whole()] + [pl.BlockSpec(memory_space=pl.ANY)] * 6,
-        out_specs=whole(),
+        functools.partial(expert_kernel, len(sums)),
+        out_shape=(jax.ShapeDtypeStruct((rows, width), dtype), jax.ShapeDtypeStruct((1, RIDER), F32)),
+        in_specs=[whole()] * (1 + len(sums)) + [pl.BlockSpec(memory_space=pl.ANY)] * 6,
+        out_specs=(whole(), whole()),
         scratch_shapes=[
             pltpu.VMEM((4, width, hid), BF16),
             pltpu.VMEM((2 * hid, width), BF16),
             pltpu.SemaphoreType.DMA((6,)),
         ],
+        compiler_params=pltpu.CompilerParams(vmem_limit_bytes=14 << 20),
         cost_estimate=pl.CostEstimate(
             flops=12 * rows * width * hid, bytes_accessed=12 * width * hid, transcendentals=rows * 2 * hid
         ),
-        compiler_params=pltpu.CompilerParams(vmem_limit_bytes=12 << 20),
         name="expert",
-    )(x, *operands)
-
-
-def join_kernel(own_ref, rider_ref, *refs):
+    )(x, *sums, *operands)
+
+
+def join_kernel(own_ref, sum_ref, twin_ref, *refs):
     backs, out_ref = refs[:-1], refs[-1]
     width = own_ref.shape[1]
     first = 0
     for back in backs:
-        span = pl.ds(first, back.shape[0])
-        out_ref[span, :width] = (own_ref[span, :] + back[...].astype(F32)).astype(BF16)
-        first += back.shape[0]
-    even = (iota((ROWS, RIDER), 0) & 1) == 0
-    out_ref[:, width:] = jnp.where(even, rider_ref[...], 0.0).astype(BF16)
-
-
-def join(own, rider, backs):
+        many = back.shape[0]
+        both = (own_ref[pl.ds(first, many), :] + back[...].astype(F32)).astype(BF16)
+        out_ref[pl.ds(first // CAP, many // CAP), :, :width] = both.reshape(many // CAP, CAP, width)
+        first += many
+    shape = (ROWS, RIDER)
+    value = jnp.broadcast_to(sum_ref[...] + twin_ref[...], shape)
+    keep = ((iota(shape, 0) & 1) == 0) & (iota(shape, 1) < TERMS)
+    rider = jnp.zeros(shape, F32)
+    for i, term in enumerate(split3(value)):
+        term = jnp.where(keep, term.astype(F32), 0.0)
+        rider = rider + (pltpu.roll(term, i * TERMS, 1) if i else term)
+    out_ref[:, :, width:] = rider.astype(BF16).reshape(MEMBERS, CAP, RIDER)
+
+
+def join(own, total, twin, backs):
     return pl.pallas_call(
         join_kernel,
-        out_shape=jax.ShapeDtypeStruct((ROWS, own.shape[1] + RIDER), BF16),
-        in_specs=[whole()] * (2 + len(backs)),
+        out_shape=jax.ShapeDtypeStruct((MEMBERS, CAP, own.shape[1] + RIDER), BF16),
+        in_specs=[whole()] * (3 + len(backs)),
         out_specs=whole(),
-        compiler_params=pltpu.CompilerParams(vmem_limit_bytes=6 << 20),
+        compiler_params=pltpu.CompilerParams(vmem_limit_bytes=8 << 20),
         name="join",
-    )(own, rider, *backs)
+    )(own, total, twin, *backs)
 
 
 def combine_kernel(side_ref, rows_ref, scale_ref, out_ref, mass_ref):
     side = side_ref[0]
     tok, width = out_ref.shape
     weight = scale_ref[:, :ROWS]
-    parts = jnp.dot(weight, rows_ref[:, :width], preferred_element_type=F32)
+    rows = rows_ref[...].reshape(ROWS, -1)
+    parts = jnp.dot(weight, rows[:, :width], preferred_element_type=F32)
     out_ref[...] = (parts[:tok] + parts[tok : 2 * tok] + parts[2 * tok :]).astype(BF16)
     lane, e = iota((RIDER, EXPERTS_ALL), 0), iota((RIDER, EXPERTS_ALL), 1)
     within = e - SLICE * by_slice(e)
-    same = (lane == within) | (lane == within + SLICE) | (lane == within + 2 * SLICE)
-    total = jnp.dot(rows_ref[:, width:], jnp.where(same, 1.0, 0.0).astype(BF16), preferred_element_type=F32)
+    same = (lane - SLICE * by_slice(lane) == within) & (lane < 3 * TERMS)
+    total = jnp.dot(rows[:, width:], jnp.where(same, 1.0, 0.0).astype(BF16), preferred_element_type=F32)
     row, e2 = iota((ROWS, EXPERTS_ALL), 0), iota((ROWS, EXPERTS_ALL), 1)
     mine = ((row & 1) == 0) & (slice_of(row >> 1, side) == by_slice(e2))
     mass_ref[...] = jnp.sum(jnp.where(mine, total, 0.0), axis=0)
 
 
 def combine(side, rows, scale, tok):
-    width = rows.shape[1] - RIDER
+    width = rows.shape[2] - RIDER
     return pl.pallas_call(
         combine_kernel,
         out_shape=(jax.ShapeDtypeStruct((tok, width), BF16), jax.ShapeDtypeStruct((EXPERTS_ALL,), F32)),
@@ -237,9 +252,8 @@
     )(side, rows, scale)
 
 
-def far(rows):
-    blocks = rows.reshape(MEMBERS, CAP, rows.shape[1])
-    return lax.all_to_all(blocks, "exp", 0, 0, axis_index_groups=FAR, tiled=True).reshape(rows.shape)
+def far(blocks):
+    return lax.all_to_all(blocks, "exp", 0, 0, axis_index_groups=FAR, tiled=True)
 
 
 def shards(tokens, expert_ids, gate_scores, gate_weight, up_weight, down_weight):
@@ -250,18 +264,15 @@
     side = ((ring & 1) ^ (ring >> 3)).astype(I32).reshape(1)
     out, scale = pack(side, tokens, expert_ids, gate_scores)
     mine = far(out)
-    step = ROWS // CHUNKS
+    step = MEMBERS // CHUNKS
     theirs = [lax.ppermute(mine[i * step : (i + 1) * step], "exp", BESIDE) for i in range(CHUNKS)]
-    own = expert(mine, weights, twins, F32)
-    partials = [expert(x, weights, twins, BF16) for x in theirs]
-    backs = [lax.ppermute(p, "exp", BESIDE) for p in partials]
-    part = sum(jnp.sum(x[:, width:], axis=0, dtype=F32) for x in [mine] + theirs)
-    part = jnp.sum(part[: 3 * SLICE].reshape(3, SLICE), axis=0, keepdims=True)
-    part, _ = lax.optimization_barrier((part, partials[-1]))
-    part = part + lax.ppermute(part, "exp", TWIN)
-    rider = jnp.concatenate([t.astype(F32) for t in split3(part)], axis=1)
-    rider = jnp.pad(rider, ((0, 0), (0, RIDER - 3 * SLICE)))
-    returned = far(join(own, rider, backs))
+    backs, total = [], []
+    for x in theirs:
+        partial, summed = expert(x, total, weights, twins, BF16)
+        backs.append(lax.ppermute(partial, "exp", BESIDE))
+        total = [summed]
+    own, total = expert(mine, total, weights, twins, F32)
+    returned = far(join(own, total, lax.ppermute(total, "exp", TWIN), backs))
     combined, mass = combine(side, returned, scale, tok_rows)
     return combined, mass
 

time: 121 us -> 115 us (0.950); the launches traced: 119 us -> 115 us
  waiting for transfers between devices: 32.7 us -> 24.9 us
  starting transfers between devices: 32.6 us -> 37.8 us
  local copies, waits for them, and re-layouts: 6.38 us -> 3.9 us
  Pallas kernels: 9.49 us -> 11.1 us
    ppermute x1 -> x2, waiting for transfers between devices: 10.4 us -> 3.93 us  [shards(): lax.ppermute(mine[i * step:(i + 1) * step], 'exp', BESIDE)]
    ppermute x1 -> x2, starting transfers between devices: 2.76 us -> 5.84 us  [shards(): lax.ppermute(mine[i * step:(i + 1) * step], 'exp', BESIDE)]
    reshape x5 -> x0, local copies, waits for them, and re-layouts: 2.63 us -> none  [the longest x2 1.38 us: far(): lax.all_to_all(blocks, 'exp', 0, 0, axis_index_groups=FAR, tiled=True)]
    ppermute x2 -> x3, starting transfers between devices: 5.56 us -> 7.76 us  [the longest x2 5.84 us: shards(): backs.append(lax.ppermute(partial, 'exp', BESIDE))]
    pallas_call x4 -> x5, Pallas kernels: 8.42 us -> 10.1 us  [the longest x3 7.98 us: expert(): pl.pallas_call(functools.partial(expert_kernel, len(sums)), out_shape=(ja...]
    ppermute x2 -> x3, waiting for transfers between devices: 3.67 us -> 2.36 us  [the longest x2 1.23 us: shards(): backs.append(lax.ppermute(partial, 'exp', BESIDE))]
    unnamed x16 -> x14, local copies, waits for them, and re-layouts: 3.75 us -> 3.57 us
  transfers between devices with their start and end apart: 7 -> 9, of which waited for: 4 -> 4; matrix products, arithmetic and copies ran while one was open for 1% -> 0% of each run, Pallas kernels for 2% -> 5%
where the time goes in v4:
time: 115 us
  starting transfers between devices  37.8 us (33%)
  blocking collectives  36.1 us (31%)
  waiting for transfers between devices  24.9 us (22%)
  Pallas kernels  11.1 us (10%)
  local copies, waits for them, and re-layouts  3.9 us (3%)
    all_to_all x1, blocking collectives, far(): lax.all_to_all(blocks, 'exp', 0, 0, axis_index_groups=FAR, tiled=True)  36.1 us
    all_to_all x1, waiting for transfers between devices, far(): lax.all_to_all(blocks, 'exp', 0, 0, axis_index_groups=FAR, tiled=True)  18.6 us
    all_to_all x1, starting transfers between devices, far(): lax.all_to_all(blocks, 'exp', 0, 0, axis_index_groups=FAR, tiled=True)  18 us
    pallas_call x3, Pallas kernels, expert(): pl.pallas_call(functools.partial(expert_kernel, len(sums)), out_shape=(ja...  7.98 us
    ppermute x3, starting transfers between devices, shards(): twins = tuple((lax.ppermute(w, 'exp', TWIN) for w in weights))  6.25 us
    ppermute x2, starting transfers between devices, shards(): lax.ppermute(mine[i * step:(i + 1) * step], 'exp', BESIDE)  5.84 us
    ppermute x2, starting transfers between devices, shards(): backs.append(lax.ppermute(partial, 'exp', BESIDE))  5.84 us
    ppermute x2, waiting for transfers between devices, shards(): lax.ppermute(mine[i * step:(i + 1) * step], 'exp', BESIDE)  3.93 us
  transfers between devices with their start and end apart: 9, of which 4 were waited for; matrix products, arithmetic and copies ran while one was open for 0% of the time, Pallas kernels for 5%

profile of v4, /device:TPU:24, one launch (start us, length us, event | category | flops | bytes accessed | tf_op | source)
XLA Modules:
  0.0 114.7 jit_solution(10235001722796284345)
XLA Ops:
  0.6 0.0 copy-start
  0.7 0.0 copy-start.4
  0.7 1.0 copy-done.4
  1.7 0.0 copy-start.5
  1.7 0.7 copy-done.5
  2.4 0.0 copy-start.6
  2.4 0.7 copy-done.6
  3.1 1.9 %pack.1 = (bf16[32,2,3712]{2,1,0:T(2,128)(2,1)}, bf16[96,128]{1,0:T(8,128)(2,1)S(1)}) custom-call(s32[1]{0:T(128)} %bitcast.side_ref, bf16[32,3584]{1,0:T(8,128)(2,1)S(1)} %copy-done.4, s32[8,32]{1,0:T(8,128)S(1)} %bitcast.3, f32[8,32]{1,0:T(8,128)S(1)} %bitcast.4), custom_call_target="tpu_custom_call" | custom-call | tf_op jit(solution)/shard_map/pack/pallas_call | solution.py:131
  4.9 0.0 copy-start.1
  4.9 18.0 %all-to-all-start = ((bf16[32,2,3712]{2,1,0:T(2,128)(2,1)}), bf16[32,2,3712]{2,1,0:T(2,128)(2,1)S(1)}, u32[]{:S(2)}, u32[]{:S(2)}) async-start(bf16[32,2,3712]{2,1,0:T(2,128)(2,1)} %get-tuple-element.10), calls=%async_computation | async-start | bytes 950272 | tf_op jit(solution)/shard_map/all_to_all | solution.py:256
  22.9 0.0 copy-done
  22.9 1.9 %collective-permute-start.2 = (bf16[3584,128]{1,0:T(8,128)(2,1)S(1)}, bf16[3584,128]{1,0:T(8,128)(2,1)S(1)}, u32[]{:S(2)}, u32[]{:S(2)}) collective-permute-start(bf16[3584,128]{1,0:T(8,128)(2,1)S(1)} %copy-done), channel_id=1, source_target_pairs={{0,1},{1,0},{2,3},{3,2},{4,5},{5,4},{6,7},{7,6},{8,9},{9,8},{10,11... | collective-permute-start | bytes 2752520 | tf_op jit(solution)/shard_map/ppermute | solution.py:262
  24.8 2.4 %collective-permute-start.3 = (bf16[3584,128]{1,0:T(8,128)(2,1)}, bf16[3584,128]{1,0:T(8,128)(2,1)}, u32[]{:S(2)}, u32[]{:S(2)}) collective-permute-start(bf16[3584,128]{1,0:T(8,128)(2,1)} %refs_3_.3), channel_id=1, source_target_pairs={{0,1},{1,0},{2,3},{3,2},{4,5},{5,4},{6,7},{7,6},{8,9},{9,8},{10,11... | collective-permute-start | bytes 2752520 | tf_op jit(solution)/shard_map/ppermute | solution.py:262
  27.3 1.9 %collective-permute-start.4 = (bf16[128,3584]{1,0:T(8,128)(2,1)}, bf16[128,3584]{1,0:T(8,128)(2,1)}, u32[]{:S(2)}, u32[]{:S(2)}) collective-permute-start(bf16[128,3584]{1,0:T(8,128)(2,1)} %refs_5_.3), channel_id=1, source_target_pairs={{0,1},{1,0},{2,3},{3,2},{4,5},{5,4},{6,7},{7,6},{8,9},{9,8},{10,11... | collective-permute-start | bytes 2752520 | tf_op jit(solution)/shard_map/ppermute | solution.py:262
  29.2 18.6 %all-to-all-done.x_ref = bf16[32,2,3712]{2,1,0:T(2,128)(2,1)S(1)} async-done(((bf16[32,2,3712]{2,1,0:T(2,128)(2,1)}), bf16[32,2,3712]{2,1,0:T(2,128)(2,1)S(1)}, u32[]{:S(2)}, u32[]{:S(2)}) %all-to-all-start) | async-done | bytes 475168 | tf_op jit(solution)/shard_map/all_to_all | solution.py:256
  47.8 0.3 fusion
  48.1 2.8 %collective-permute-start.1 = (bf16[16,2,3712]{2,1,0:T(2,128)(2,1)S(1)}, bf16[16,2,3712]{2,1,0:T(2,128)(2,1)S(1)}, u32[]{:S(2)}, u32[]{:S(2)}) collective-permute-start(bf16[16,2,3712]{2,1,0:T(2,128)(2,1)S(1)} %get-tuple-element.18), channel_id=1, source_target_pairs={{0,2},{1,3},{2,0},{3,1},{4,6},{5,7},{6,4},{7,5},{8,10},{9,11},{10,... | collective-permute-start | bytes 712712 | tf_op jit(solution)/shard_map/ppermute | solution.py:268
  50.9 3.1 %collective-permute-start = (bf16[16,2,3712]{2,1,0:T(2,128)(2,1)S(1)}, bf16[16,2,3712]{2,1,0:T(2,128)(2,1)S(1)}, u32[]{:S(2)}, u32[]{:S(2)}) collective-permute-start(bf16[16,2,3712]{2,1,0:T(2,128)(2,1)S(1)} %get-tuple-element.19), channel_id=1, source_target_pairs={{0,2},{1,3},{2,0},{3,1},{4,6},{5,7},{6,4},{7,5},{8,10},{9,11},{10,... | collective-permute-start | bytes 712712 | tf_op jit(solution)/shard_map/ppermute | solution.py:268
  54.0 0.0 collective-permute-done.2.refs_1_.refs_2_
  54.0 0.0 collective-permute-done.3.refs_3_.refs_4_
  54.0 0.0 collective-permute-done.4.refs_5_.refs_6_
  54.0 3.9 %collective-permute-done.1.x_ref = bf16[16,2,3712]{2,1,0:T(2,128)(2,1)S(1)} collective-permute-done((bf16[16,2,3712]{2,1,0:T(2,128)(2,1)S(1)}, bf16[16,2,3712]{2,1,0:T(2,128)(2,1)S(1)}, u32[]{:S(2)}, u32[]{:S(2)}) %collective-permute-start.1) | collective-permute-done | bytes 237600 | tf_op jit(solution)/shard_map/ppermute | solution.py:268
  57.9 0.0 copy-done.1
  57.9 0.0 copy-start.2
  57.9 1.2 %copy-done.2 = bf16[128,3584]{1,0:T(8,128)(2,1)S(1)} copy-done((bf16[128,3584]{1,0:T(8,128)(2,1)S(1)}, bf16[128,3584]{1,0:T(8,128)(2,1)}, u32[]{:S(2)}) %copy-start.2) | copy-done | bytes 917528
  59.1 0.0 copy-start.3
  59.1 2.6 %expert.3 = (bf16[32,3584]{1,0:T(8,128)(2,1)S(1)}, f32[1,128]{1,0:T(1,128)S(1)}) custom-call(bf16[16,2,3712]{2,1,0:T(2,128)(2,1)S(1)} %collective-permute-done.1.x_ref, bf16[3584,128]{1,0:T(8,128)(2,1)S(1)} %copy-done, bf16[3584,128]{1,0:T(8,128)(2,1)S(1)} %collective-permute-done.2.refs_1_.refs_2_, bf16[3584,128]{1,0:T(8,128)(2,1)S(1)} %copy-done.1, ...), custom_call_target="tpu_custom_call" | custom-call | flops 176160768 | bytes 5505024 | tf_op jit(solution)/shard_map/expert/pallas_call | solution.py:179
  61.8 0.0 collective-permute-done.x_ref
  61.8 0.0 copy-done.3
  61.8 2.7 %expert.4 = (bf16[32,3584]{1,0:T(8,128)(2,1)S(1)}, f32[1,128]{1,0:T(1,128)S(1)}) custom-call(bf16[16,2,3712]{2,1,0:T(2,128)(2,1)S(1)} %collective-permute-done.x_ref, f32[1,128]{1,0:T(1,128)S(1)} %get-tuple-element.11.refs_0_, bf16[3584,128]{1,0:T(8,128)(2,1)S(1)} %copy-done, bf16[3584,128]{1,0:T(8,128)(2,1)S(1)} %collective-permute-done.2.refs_1_.refs_2_, ...), custom_call_target="tpu_custom_call" | custom-call | flops 176160768 | bytes 5505024 | tf_op jit(solution)/shard_map/expert/pallas_call | solution.py:179
  64.5 3.5 %collective-permute-start.7 = (bf16[32,3584]{1,0:T(8,128)(2,1)S(1)}, bf16[32,3584]{1,0:T(8,128)(2,1)S(1)}, u32[]{:S(2)}, u32[]{:S(2)}) collective-permute-start(bf16[32,3584]{1,0:T(8,128)(2,1)S(1)} %get-tuple-element.16), channel_id=1, source_target_pairs={{0,2},{1,3},{2,0},{3,1},{4,6},{5,7},{6,4},{7,5},{8,10},{9,11},{10,... | collective-permute-start | bytes 688136 | tf_op jit(solution)/shard_map/ppermute | solution.py:272
  68.0 2.3 %collective-permute-start.6 = (bf16[32,3584]{1,0:T(8,128)(2,1)S(1)}, bf16[32,3584]{1,0:T(8,128)(2,1)S(1)}, u32[]{:S(2)}, u32[]{:S(2)}) collective-permute-start(bf16[32,3584]{1,0:T(8,128)(2,1)S(1)} %get-tuple-element.15), channel_id=1, source_target_pairs={{0,2},{1,3},{2,0},{3,1},{4,6},{5,7},{6,4},{7,5},{8,10},{9,11},{10,... | collective-permute-start | bytes 688136 | tf_op jit(solution)/shard_map/ppermute | solution.py:272
  70.3 2.7 %expert.5 = (f32[64,3584]{1,0:T(8,128)S(1)}, f32[1,128]{1,0:T(1,128)S(1)}) custom-call(bf16[32,2,3712]{2,1,0:T(2,128)(2,1)S(1)} %all-to-all-done.x_ref, f32[1,128]{1,0:T(1,128)S(1)} %get-tuple-element.12.refs_0_, bf16[3584,128]{1,0:T(8,128)(2,1)S(1)} %copy-done, bf16[3584,128]{1,0:T(8,128)(2,1)S(1)} %collective-permute-done.2.refs_1_.refs_2_, ...), custom_call_target="tpu_custom_call" | custom-call | flops 352321536 | bytes 5505024 | tf_op jit(solution)/shard_map/expert/pallas_call | solution.py:179
  73.0 1.9 %collective-permute-start.5 = (f32[1,128]{1,0:T(1,128)S(1)}, f32[1,128]{1,0:T(1,128)S(1)}, u32[]{:S(2)}, u32[]{:S(2)}) collective-permute-start(f32[1,128]{1,0:T(1,128)S(1)} %get-tuple-element.14.sum_ref), channel_id=1, source_target_pairs={{0,1},{1,0},{2,3},{3,2},{4,5},{5,4},{6,7},{7,6},{8,9},{9,8},{10,11... | collective-permute-start | bytes 1544 | tf_op jit(solution)/shard_map/ppermute | solution.py:275
  74.9 1.1 collective-permute-done.5.twin_ref
  76.1 0.0 collective-permute-done.7.refs_1_
  76.1 1.2 %collective-permute-done.6.refs_0_ = bf16[32,3584]{1,0:T(8,128)(2,1)S(1)} collective-permute-done((bf16[32,3584]{1,0:T(8,128)(2,1)S(1)}, bf16[32,3584]{1,0:T(8,128)(2,1)S(1)}, u32[]{:S(2)}, u32[]{:S(2)}) %collective-permute-start.6) | collective-permute-done | bytes 229408 | tf_op jit(solution)/shard_map/ppermute | solution.py:272
  77.3 0.2 join.1
  77.5 36.1 %all_to_all.10.rows_ref = bf16[32,2,3712]{2,1,0:T(2,128)(2,1)S(1)} all-to-all(bf16[32,2,3712]{2,1,0:T(2,128)(2,1)S(1)} %join.1), channel_id=1, replica_groups={{26,30,0,4,8,12,18,22,58,62,32,36,40,44,50,54,90,94,64,68,72,76,82,86,1..., dimensions={0} | all-to-all | bytes 950272 | tf_op jit(solution)/shard_map/all_to_all | solution.py:256
  113.6 1.0 combine.1
Async XLA Ops:
  0.6 22.3 %copy-start = (bf16[3584,128]{1,0:T(8,128)(2,1)S(1)}, bf16[3584,128]{1,0:T(8,128)(2,1)}, u32[]{:S(2)}) copy-start(bf16[3584,128]{1,0:T(8,128)(2,1)} %refs_1_.3) | copy-start | bytes 2752516
  0.7 1.0 copy-start.4
  1.7 0.7 copy-start.5
  2.4 0.7 copy-start.6
  4.9 53.0 %copy-start.1 = (bf16[3584,128]{1,0:T(8,128)(2,1)S(1)}, bf16[3584,128]{1,0:T(8,128)(2,1)}, u32[]{:S(2)}) copy-start(bf16[3584,128]{1,0:T(8,128)(2,1)} %refs_3_.3) | copy-start | bytes 2752516
  4.9 42.9 %all-to-all-start = ((bf16[32,2,3712]{2,1,0:T(2,128)(2,1)}), bf16[32,2,3712]{2,1,0:T(2,128)(2,1)S(1)}, u32[]{:S(2)}, u32[]{:S(2)}) async-start(bf16[32,2,3712]{2,1,0:T(2,128)(2,1)} %get-tuple-element.10), calls=%async_computation | async-start | bytes 950272 | tf_op jit(solution)/shard_map/all_to_all | solution.py:256
  22.9 31.1 %collective-permute-start.2 = (bf16[3584,128]{1,0:T(8,128)(2,1)S(1)}, bf16[3584,128]{1,0:T(8,128)(2,1)S(1)}, u32[]{:S(2)}, u32[]{:S(2)}) collective-permute-start(bf16[3584,128]{1,0:T(8,128)(2,1)S(1)} %copy-done), channel_id=1, source_target_pairs={{0,1},{1,0},{2,3},{3,2},{4,5},{5,4},{6,7},{7,6},{8,9},{9,8},{10,11... | collective-permute-start | bytes 2752520 | tf_op jit(solution)/shard_map/ppermute | solution.py:262
  24.8 29.1 %collective-permute-start.3 = (bf16[3584,128]{1,0:T(8,128)(2,1)}, bf16[3584,128]{1,0:T(8,128)(2,1)}, u32[]{:S(2)}, u32[]{:S(2)}) collective-permute-start(bf16[3584,128]{1,0:T(8,128)(2,1)} %refs_3_.3), channel_id=1, source_target_pairs={{0,1},{1,0},{2,3},{3,2},{4,5},{5,4},{6,7},{7,6},{8,9},{9,8},{10,11... | collective-permute-start | bytes 2752520 | tf_op jit(solution)/shard_map/ppermute | solution.py:262
  27.3 26.7 %collective-permute-start.4 = (bf16[128,3584]{1,0:T(8,128)(2,1)}, bf16[128,3584]{1,0:T(8,128)(2,1)}, u32[]{:S(2)}, u32[]{:S(2)}) collective-permute-start(bf16[128,3584]{1,0:T(8,128)(2,1)} %refs_5_.3), channel_id=1, source_target_pairs={{0,1},{1,0},{2,3},{3,2},{4,5},{5,4},{6,7},{7,6},{8,9},{9,8},{10,11... | collective-permute-start | bytes 2752520 | tf_op jit(solution)/shard_map/ppermute | solution.py:262
  48.1 9.8 %collective-permute-start.1 = (bf16[16,2,3712]{2,1,0:T(2,128)(2,1)S(1)}, bf16[16,2,3712]{2,1,0:T(2,128)(2,1)S(1)}, u32[]{:S(2)}, u32[]{:S(2)}) collective-permute-start(bf16[16,2,3712]{2,1,0:T(2,128)(2,1)S(1)} %get-tuple-element.18), channel_id=1, source_target_pairs={{0,2},{1,3},{2,0},{3,1},{4,6},{5,7},{6,4},{7,5},{8,10},{9,11},{10,... | collective-permute-start | bytes 712712 | tf_op jit(solution)/shard_map/ppermute | solution.py:268
  50.9 10.9 %collective-permute-start = (bf16[16,2,3712]{2,1,0:T(2,128)(2,1)S(1)}, bf16[16,2,3712]{2,1,0:T(2,128)(2,1)S(1)}, u32[]{:S(2)}, u32[]{:S(2)}) collective-permute-start(bf16[16,2,3712]{2,1,0:T(2,128)(2,1)S(1)} %get-tuple-element.19), channel_id=1, source_target_pairs={{0,2},{1,3},{2,0},{3,1},{4,6},{5,7},{6,4},{7,5},{8,10},{9,11},{10,... | collective-permute-start | bytes 712712 | tf_op jit(solution)/shard_map/ppermute | solution.py:268
  57.9 1.2 %copy-start.2 = (bf16[128,3584]{1,0:T(8,128)(2,1)S(1)}, bf16[128,3584]{1,0:T(8,128)(2,1)}, u32[]{:S(2)}) copy-start(bf16[128,3584]{1,0:T(8,128)(2,1)} %refs_5_.3) | copy-start | bytes 2752516
  59.1 2.7 %copy-start.3 = (bf16[128,3584]{1,0:T(8,128)(2,1)S(1)}, bf16[128,3584]{1,0:T(8,128)(2,1)}, u32[]{:S(2)}) copy-start(bf16[128,3584]{1,0:T(8,128)(2,1)} %refs_5_.3) | copy-start | bytes 2752516
  64.5 11.6 %collective-permute-start.7 = (bf16[32,3584]{1,0:T(8,128)(2,1)S(1)}, bf16[32,3584]{1,0:T(8,128)(2,1)S(1)}, u32[]{:S(2)}, u32[]{:S(2)}) collective-permute-start(bf16[32,3584]{1,0:T(8,128)(2,1)S(1)} %get-tuple-element.16), channel_id=1, source_target_pairs={{0,2},{1,3},{2,0},{3,1},{4,6},{5,7},{6,4},{7,5},{8,10},{9,11},{10,... | collective-permute-start | bytes 688136 | tf_op jit(solution)/shard_map/ppermute | solution.py:272
  68.0 9.3 %collective-permute-start.6 = (bf16[32,3584]{1,0:T(8,128)(2,1)S(1)}, bf16[32,3584]{1,0:T(8,128)(2,1)S(1)}, u32[]{:S(2)}, u32[]{:S(2)}) collective-permute-start(bf16[32,3584]{1,0:T(8,128)(2,1)S(1)} %get-tuple-element.15), channel_id=1, source_target_pairs={{0,2},{1,3},{2,0},{3,1},{4,6},{5,7},{6,4},{7,5},{8,10},{9,11},{10,... | collective-permute-start | bytes 688136 | tf_op jit(solution)/shard_map/ppermute | solution.py:272
  73.0 3.1 %collective-permute-start.5 = (f32[1,128]{1,0:T(1,128)S(1)}, f32[1,128]{1,0:T(1,128)S(1)}, u32[]{:S(2)}, u32[]{:S(2)}) collective-permute-start(f32[1,128]{1,0:T(1,128)S(1)} %get-tuple-element.14.sum_ref), channel_id=1, source_target_pairs={{0,1},{1,0},{2,3},{3,2},{4,5},{5,4},{6,7},{7,6},{8,9},{9,8},{10,11... | collective-permute-start | bytes 1544 | tf_op jit(solution)/shard_map/ppermute | solution.py:275

commit v5 on v4

--- a/solution.py
+++ b/solution.py
@@ -7,8 +7,8 @@
 from jax.experimental.pallas import tpu as pltpu
 from jax.sharding import PartitionSpec as P
 
+
 EXPERTS_ALL = 384
-EXPERTS = 8
 CAP = 2
 COLS, RINGS, CORES = 4, 16, 2
 PAIRS = RINGS // 2
@@ -36,7 +36,6 @@
 
 FAR = far_groups()
 MEMBERS = COLS * PAIRS
-SPREAD = MEMBERS // EXPERTS
 ROWS = MEMBERS * CAP
 BESIDE = [(i, i ^ CORES) for i in range(COLS * RINGS * CORES)]
 TWIN = [(i, i ^ 1) for i in range(COLS * RINGS * CORES)]
@@ -79,14 +78,21 @@
     return pl.BlockSpec(memory_space=pltpu.SMEM)
 
 
-def pack_kernel(side_ref, tok_hbm, ids_ref, score_ref, out_ref, scale_ref, tok_ref, flip_ids, flip_score, sem):
-    fetch = pltpu.make_async_copy(tok_hbm, tok_ref, sem)
-    fetch.start()
+def pack_kernel(side_ref, tok_hbm, ids_hbm, score_hbm, out_ref, scale_ref, tok_ref, ids_ref, score_ref, flip_ids, flip_score, sems):
+    fetch = pltpu.make_async_copy(tok_hbm, tok_ref, sems.at[0])
+    small = [
+        pltpu.make_async_copy(ids_hbm, ids_ref, sems.at[1]),
+        pltpu.make_async_copy(score_hbm, score_ref, sems.at[2]),
+    ]
+    for copy in small + [fetch]:
+        copy.start()
     side = side_ref[0]
     rows, width = tok_ref.shape
     top = ids_ref.shape[0]
     flip_ids[...] = jnp.zeros_like(flip_ids)
     flip_score[...] = jnp.zeros_like(flip_score)
+    for copy in small:
+        copy.wait()
     flip_ids[:top, :rows] = ids_ref[...]
     flip_score[:top, :rows] = score_ref[...]
     ids, score = flip_ids[...].T[:rows], flip_score[...].T[:rows]
@@ -134,42 +140,42 @@
             jax.ShapeDtypeStruct((MEMBERS, CAP, width + RIDER), BF16),
             jax.ShapeDtypeStruct((3 * rows, 128), BF16),
         ),
-        in_specs=[scalar(), pl.BlockSpec(memory_space=pl.ANY), whole(), whole()],
+        in_specs=[scalar()] + [pl.BlockSpec(memory_space=pl.ANY)] * 3,
         out_specs=(whole(), whole()),
         scratch_shapes=[
             pltpu.VMEM((rows, width), BF16),
+            pltpu.VMEM(ids.shape[::-1], I32),
+            pltpu.VMEM(scores.shape[::-1], F32),
             pltpu.VMEM((128, 128), I32),
             pltpu.VMEM((128, 128), F32),
-            pltpu.SemaphoreType.DMA(()),
+            pltpu.SemaphoreType.DMA((3,)),
         ],
-        compiler_params=pltpu.CompilerParams(vmem_limit_bytes=6 << 20),
+        compiler_params=pltpu.CompilerParams(vmem_limit_bytes=60 << 20),
         name="pack",
     )(side, tokens, ids.T, scores.T)
 
 
 def expert_kernel(n_sums, x_ref, *refs):
-    sums, hbm, (out_ref, sum_ref, wide, down, sems) = refs[:n_sums], refs[n_sums : n_sums + 6], refs[n_sums + 6 :]
-    width, hid = hbm[0].shape
-    targets = [wide.at[i] for i in range(4)] + [down.at[pl.ds(i * hid, hid), :] for i in range(2)]
-    copies = [pltpu.make_async_copy(ref, buf, sems.at[i]) for i, (ref, buf) in enumerate(zip(hbm, targets))]
-    for copy in copies:
-        copy.start()
+    sums, mats, (out_ref, sum_ref) = refs[:n_sums], refs[n_sums : n_sums + 6], refs[n_sums + 6 :]
+    width, hid = mats[0].shape
     rows = x_ref[...].reshape(-1, x_ref.shape[-1])
     x = rows[:, :width]
     total = jnp.sum(rows[:, width:].astype(F32), axis=0, keepdims=True)
     for other in sums:
-        total = total + other[...]
+        if other.shape[0] == 1:
+            total = total + other[...]
+        else:
+            more = other[...].reshape(-1, other.shape[-1])[:, width:]
+            total = total + jnp.sum(more.astype(F32), axis=0, keepdims=True)
     sum_ref[...] = total
     act = []
     for i in range(4):
-        copies[i].wait()
-        act.append(jnp.dot(x, wide[i], preferred_element_type=F32))
+        act.append(jnp.dot(x, mats[i][...], preferred_element_type=F32))
     g = jnp.concatenate(act[:2], axis=1)
     u = jnp.concatenate(act[2:], axis=1)
     h = (g / (1.0 + jnp.exp(-g)) * u).astype(BF16)
-    copies[4].wait()
-    copies[5].wait()
-    out_ref[...] = jnp.dot(h, down[...], preferred_element_type=F32).astype(out_ref.dtype)
+    out = [jnp.dot(h[:, i * hid : (i + 1) * hid], mats[4 + i][...], preferred_element_type=F32) for i in range(2)]
+    out_ref[...] = (out[0] + out[1]).astype(out_ref.dtype)
 
 
 def expert(x, sums, weights, twins, dtype):
@@ -179,19 +185,54 @@
     return pl.pallas_call(
         functools.partial(expert_kernel, len(sums)),
         out_shape=(jax.ShapeDtypeStruct((rows, width), dtype), jax.ShapeDtypeStruct((1, RIDER), F32)),
-        in_specs=[whole()] * (1 + len(sums)) + [pl.BlockSpec(memory_space=pl.ANY)] * 6,
+        in_specs=[whole()] * (7 + len(sums)),
         out_specs=(whole(), whole()),
-        scratch_shapes=[
-            pltpu.VMEM((4, width, hid), BF16),
-            pltpu.VMEM((2 * hid, width), BF16),
-            pltpu.SemaphoreType.DMA((6,)),
-        ],
         compiler_params=pltpu.CompilerParams(vmem_limit_bytes=14 << 20),
         cost_estimate=pl.CostEstimate(
             flops=12 * rows * width * hid, bytes_accessed=12 * width * hid, transcendentals=rows * 2 * hid
         ),
         name="expert",
     )(x, *sums, *operands)
+
+
+def hold_kernel(*refs):
+    n = len(refs) // 2
+    sems = refs[-1]
+    copies = [pltpu.make_async_copy(refs[i], refs[n + i], sems.at[i]) for i in range(n)]
+    for copy in copies:
+        copy.start()
+    for copy in copies:
+        copy.wait()
+
+
+def hold(weights):
+    return pl.pallas_call(
+        hold_kernel,
+        out_shape=tuple(jax.ShapeDtypeStruct(w.shape, w.dtype) for w in weights),
+        in_specs=[pl.BlockSpec(memory_space=pl.ANY)] * len(weights),
+        out_specs=(whole(),) * len(weights),
+        scratch_shapes=[pltpu.SemaphoreType.DMA((len(weights),))],
+        compiler_params=pltpu.CompilerParams(vmem_limit_bytes=4 << 20),
+        name="hold",
+    )(*weights)
+
+
+def cut_kernel(whole_ref, *part_refs):
+    many = part_refs[0].shape[0]
+    for i, part in enumerate(part_refs):
+        part[...] = whole_ref[pl.ds(i * many, many)]
+
+
+def cut(blocks, pieces):
+    shape = (blocks.shape[0] // pieces,) + blocks.shape[1:]
+    return pl.pallas_call(
+        cut_kernel,
+        out_shape=(jax.ShapeDtypeStruct(shape, blocks.dtype),) * pieces,
+        in_specs=[whole()],
+        out_specs=(whole(),) * pieces,
+        compiler_params=pltpu.CompilerParams(vmem_limit_bytes=3 << 20),
+        name="cut",
+    )(blocks)
 
 
 def join_kernel(own_ref, sum_ref, twin_ref, *refs):
@@ -257,22 +298,25 @@
 
 
 def shards(tokens, expert_ids, gate_scores, gate_weight, up_weight, down_weight):
-    tok_rows, width = tokens.shape
+    tok_rows, _ = tokens.shape
     weights = (gate_weight, up_weight, down_weight)
     twins = tuple(lax.ppermute(w, "exp", TWIN) for w in weights)
     ring = (lax.axis_index("exp") // CORES) % RINGS
     side = ((ring & 1) ^ (ring >> 3)).astype(I32).reshape(1)
     out, scale = pack(side, tokens, expert_ids, gate_scores)
     mine = far(out)
-    step = MEMBERS // CHUNKS
-    theirs = [lax.ppermute(mine[i * step : (i + 1) * step], "exp", BESIDE) for i in range(CHUNKS)]
+    held = hold(weights)
+    theirs = []
+    for piece in cut(mine, CHUNKS):
+        theirs.append(lax.ppermute(piece, "exp", BESIDE))
     backs, total = [], []
-    for x in theirs:
-        partial, summed = expert(x, total, weights, twins, BF16)
+    for i, x in enumerate(theirs):
+        partial, summed = expert(x, total + [mine] * (i == CHUNKS - 1), held, twins, BF16)
         backs.append(lax.ppermute(partial, "exp", BESIDE))
         total = [summed]
-    own, total = expert(mine, total, weights, twins, F32)
-    returned = far(join(own, total, lax.ppermute(total, "exp", TWIN), backs))
+    own, _ = expert(mine, [], held, twins, F32)
+    other = lax.ppermute(total[0], "exp", TWIN)
+    returned = far(join(own, total[0], other, backs))
     combined, mass = combine(side, returned, scale, tok_rows)
     return combined, mass
 

time: 115 us -> 113 us (0.983)
  local copies, waits for them, and re-layouts: 3.9 us -> 1.18 us
  Pallas kernels: 11.1 us -> 8.47 us
  blocking collectives: 36.1 us -> 37.8 us
    pallas_call x3, Pallas kernels: 7.98 us -> 3.38 us  [expert(): pl.pallas_call(functools.partial(expert_kernel, len(sums)), out_shape=(ja...]
    unnamed x14 -> x4, local copies, waits for them, and re-layouts: 3.57 us -> 1.18 us
    ppermute x2, waiting for transfers between devices: 1.23 us -> 3.59 us  [shards(): backs.append(lax.ppermute(partial, 'exp', BESIDE))]
    all_to_all x1, blocking collectives: 36.1 us -> 37.8 us  [far(): lax.all_to_all(blocks, 'exp', 0, 0, axis_index_groups=FAR, tiled=True)]
    pallas_call x0 -> x2, Pallas kernels: none -> 1.52 us  [the longest x1 1.48 us: hold(): pl.pallas_call(hold_kernel, out_shape=tuple((jax.ShapeDtypeStruct(w.shape...]
    ppermute x3, waiting for transfers between devices: 5.05 us -> 3.65 us  [the longest x2 3.65 us: shards(): theirs.append(lax.ppermute(piece, 'exp', BESIDE))]
  transfers between devices with their start and end apart: 9 -> 9, of which waited for: 4 -> 5; matrix products, arithmetic and copies ran while one was open for 0% -> 0% of each run, Pallas kernels for 5% -> 4%
where the time goes in v5:
time: 113 us; the launch traced here: 112 us
  blocking collectives  37.8 us (33%)
  starting transfers between devices  37.7 us (33%)
  waiting for transfers between devices  25.8 us (23%)
  Pallas kernels  8.47 us (7%)
  local copies, waits for them, and re-layouts  1.18 us (1%)
    all_to_all x1, blocking collectives, far(): lax.all_to_all(blocks, 'exp', 0, 0, axis_index_groups=FAR, tiled=True)  37.8 us
    all_to_all x1, waiting for transfers between devices, far(): lax.all_to_all(blocks, 'exp', 0, 0, axis_index_groups=FAR, tiled=True)  18.6 us
    all_to_all x1, starting transfers between devices, far(): lax.all_to_all(blocks, 'exp', 0, 0, axis_index_groups=FAR, tiled=True)  17.8 us
    ppermute x3, starting transfers between devices, shards(): twins = tuple((lax.ppermute(w, 'exp', TWIN) for w in weights))  6.25 us
    ppermute x2, starting transfers between devices, shards(): theirs.append(lax.ppermute(piece, 'exp', BESIDE))  5.84 us
    ppermute x2, starting transfers between devices, shards(): backs.append(lax.ppermute(partial, 'exp', BESIDE))  5.84 us
    ppermute x2, waiting for transfers between devices, shards(): theirs.append(lax.ppermute(piece, 'exp', BESIDE))  3.65 us
    ppermute x2, waiting for transfers between devices, shards(): backs.append(lax.ppermute(partial, 'exp', BESIDE))  3.59 us
  transfers between devices with their start and end apart: 9, of which 5 were waited for; matrix products, arithmetic and copies ran while one was open for 0% of the time, Pallas kernels for 4%

profile of v5, /device:TPU:24, one launch (start us, length us, event | category | flops | bytes accessed | tf_op | source)
XLA Modules:
  0.0 111.8 jit_solution(760926908875381307)
XLA Ops:
  0.7 2.3 %pack.1 = (bf16[32,2,3712]{2,1,0:T(2,128)(2,1)}, bf16[96,128]{1,0:T(8,128)(2,1)}) custom-call(s32[1]{0:T(128)} %bitcast.side_ref, bf16[32,3584]{1,0:T(8,128)(2,1)} %tok_hbm.1, s32[8,32]{1,0:T(8,128)} %bitcast.3, f32[8,32]{1,0:T(8,128)} %bitcast.4), custom_call_target="tpu_custom_call" | custom-call | tf_op jit(solution)/shard_map/pack/pallas_call | solution.py:137
  3.0 17.8 %all-to-all-start = ((bf16[32,2,3712]{2,1,0:T(2,128)(2,1)}), bf16[32,2,3712]{2,1,0:T(2,128)(2,1)S(1)}, u32[]{:S(2)}, u32[]{:S(2)}) async-start(bf16[32,2,3712]{2,1,0:T(2,128)(2,1)} %get-tuple-element.14), calls=%async_computation | async-start | bytes 950272 | tf_op jit(solution)/shard_map/all_to_all | solution.py:297
  20.8 1.9 %collective-permute-start = (bf16[3584,128]{1,0:T(8,128)(2,1)}, bf16[3584,128]{1,0:T(8,128)(2,1)S(1)}, u32[]{:S(2)}, u32[]{:S(2)}) collective-permute-start(bf16[3584,128]{1,0:T(8,128)(2,1)} %refs_0_.1), channel_id=1, source_target_pairs={{0,1},{1,0},{2,3},{3,2},{4,5},{5,4},{6,7},{7,6},{8,9},{9,8},{10,11... | collective-permute-start | bytes 2752520 | tf_op jit(solution)/shard_map/ppermute | solution.py:303
  22.8 2.4 %collective-permute-start.1 = (bf16[3584,128]{1,0:T(8,128)(2,1)}, bf16[3584,128]{1,0:T(8,128)(2,1)S(1)}, u32[]{:S(2)}, u32[]{:S(2)}) collective-permute-start(bf16[3584,128]{1,0:T(8,128)(2,1)} %refs_1_.1), channel_id=1, source_target_pairs={{0,1},{1,0},{2,3},{3,2},{4,5},{5,4},{6,7},{7,6},{8,9},{9,8},{10,11... | collective-permute-start | bytes 2752520 | tf_op jit(solution)/shard_map/ppermute | solution.py:303
  25.2 1.9 %collective-permute-start.2 = (bf16[128,3584]{1,0:T(8,128)(2,1)}, bf16[128,3584]{1,0:T(8,128)(2,1)S(1)}, u32[]{:S(2)}, u32[]{:S(2)}) collective-permute-start(bf16[128,3584]{1,0:T(8,128)(2,1)} %refs_2_.1), channel_id=1, source_target_pairs={{0,1},{1,0},{2,3},{3,2},{4,5},{5,4},{6,7},{7,6},{8,9},{9,8},{10,11... | collective-permute-start | bytes 2752520 | tf_op jit(solution)/shard_map/ppermute | solution.py:303
  27.1 18.6 %all-to-all-done.x_ref.whole_ref.refs_1_ = bf16[32,2,3712]{2,1,0:T(2,128)(2,1)S(1)} async-done(((bf16[32,2,3712]{2,1,0:T(2,128)(2,1)}), bf16[32,2,3712]{2,1,0:T(2,128)(2,1)S(1)}, u32[]{:S(2)}, u32[]{:S(2)}) %all-to-all-start) | async-done | bytes 475168 | tf_op jit(solution)/shard_map/all_to_all | solution.py:297
  45.7 2.8 %collective-permute-start.4 = (bf16[16,2,3712]{2,1,0:T(2,128)(2,1)S(1)}, bf16[16,2,3712]{2,1,0:T(2,128)(2,1)S(1)}, u32[]{:S(2)}, u32[]{:S(2)}) collective-permute-start(bf16[16,2,3712]{2,1,0:T(2,128)(2,1)S(1)} %get-tuple-element.20), channel_id=1, source_target_pairs={{0,2},{1,3},{2,0},{3,1},{4,6},{5,7},{6,4},{7,5},{8,10},{9,11},{10,... | collective-permute-start | bytes 712712 | tf_op jit(solution)/shard_map/ppermute | solution.py:311
  48.5 3.1 %collective-permute-start.3 = (bf16[16,2,3712]{2,1,0:T(2,128)(2,1)S(1)}, bf16[16,2,3712]{2,1,0:T(2,128)(2,1)S(1)}, u32[]{:S(2)}, u32[]{:S(2)}) collective-permute-start(bf16[16,2,3712]{2,1,0:T(2,128)(2,1)S(1)} %get-tuple-element.19), channel_id=1, source_target_pairs={{0,2},{1,3},{2,0},{3,1},{4,6},{5,7},{6,4},{7,5},{8,10},{9,11},{10,... | collective-permute-start | bytes 712712 | tf_op jit(solution)/shard_map/ppermute | solution.py:311
  51.6 0.0 copy-start
  51.6 1.2 %copy-done = bf16[128,3584]{1,0:T(8,128)(2,1)S(1)} copy-done((bf16[128,3584]{1,0:T(8,128)(2,1)S(1)}, bf16[128,3584]{1,0:T(8,128)(2,1)}, u32[]{:S(2)}) %copy-start) | copy-done | bytes 917528
  52.8 1.5 %hold.1 = (bf16[3584,128]{1,0:T(8,128)(2,1)S(1)}, bf16[3584,128]{1,0:T(8,128)(2,1)S(1)}, bf16[128,3584]{1,0:T(8,128)(2,1)S(1)}) custom-call(bf16[3584,128]{1,0:T(8,128)(2,1)} %refs_0_.1, bf16[3584,128]{1,0:T(8,128)(2,1)} %refs_1_.1, bf16[128,3584]{1,0:T(8,128)(2,1)S(1)} %copy-done), custom_call_target="tpu_custom_call" | custom-call | tf_op jit(solution)/shard_map/hold/pallas_call | solution.py:209
  54.3 0.0 collective-permute-done.refs_1_.refs_3_
  54.3 0.0 collective-permute-done.1.refs_3_.refs_5_
  54.3 0.0 collective-permute-done.2.refs_5_.refs_7_
  54.3 1.2 %collective-permute-done.4.x_ref = bf16[16,2,3712]{2,1,0:T(2,128)(2,1)S(1)} collective-permute-done((bf16[16,2,3712]{2,1,0:T(2,128)(2,1)S(1)}, bf16[16,2,3712]{2,1,0:T(2,128)(2,1)S(1)}, u32[]{:S(2)}, u32[]{:S(2)}) %collective-permute-start.4) | collective-permute-done | bytes 237600 | tf_op jit(solution)/shard_map/ppermute | solution.py:311
  55.5 1.0 expert.4
  56.5 2.4 %collective-permute-done.3.x_ref = bf16[16,2,3712]{2,1,0:T(2,128)(2,1)S(1)} collective-permute-done((bf16[16,2,3712]{2,1,0:T(2,128)(2,1)S(1)}, bf16[16,2,3712]{2,1,0:T(2,128)(2,1)S(1)}, u32[]{:S(2)}, u32[]{:S(2)}) %collective-permute-start.3) | collective-permute-done | bytes 237600 | tf_op jit(solution)/shard_map/ppermute | solution.py:311
  58.9 1.0 expert.5
  59.9 3.6 %collective-permute-start.7 = (bf16[32,3584]{1,0:T(8,128)(2,1)S(1)}, bf16[32,3584]{1,0:T(8,128)(2,1)S(1)}, u32[]{:S(2)}, u32[]{:S(2)}) collective-permute-start(bf16[32,3584]{1,0:T(8,128)(2,1)S(1)} %get-tuple-element.24), channel_id=1, source_target_pairs={{0,2},{1,3},{2,0},{3,1},{4,6},{5,7},{6,4},{7,5},{8,10},{9,11},{10,... | collective-permute-start | bytes 688136 | tf_op jit(solution)/shard_map/ppermute | solution.py:315
  63.5 2.2 %collective-permute-start.6 = (bf16[32,3584]{1,0:T(8,128)(2,1)S(1)}, bf16[32,3584]{1,0:T(8,128)(2,1)S(1)}, u32[]{:S(2)}, u32[]{:S(2)}) collective-permute-start(bf16[32,3584]{1,0:T(8,128)(2,1)S(1)} %get-tuple-element.23), channel_id=1, source_target_pairs={{0,2},{1,3},{2,0},{3,1},{4,6},{5,7},{6,4},{7,5},{8,10},{9,11},{10,... | collective-permute-start | bytes 688136 | tf_op jit(solution)/shard_map/ppermute | solution.py:315
  65.8 1.9 %collective-permute-start.5 = (f32[1,128]{1,0:T(1,128)S(1)}, f32[1,128]{1,0:T(1,128)S(1)}, u32[]{:S(2)}, u32[]{:S(2)}) collective-permute-start(f32[1,128]{1,0:T(1,128)S(1)} %get-tuple-element.22.sum_ref), channel_id=1, source_target_pairs={{0,1},{1,0},{2,3},{3,2},{4,5},{5,4},{6,7},{7,6},{8,9},{9,8},{10,11... | collective-permute-start | bytes 1544 | tf_op jit(solution)/shard_map/ppermute | solution.py:318
  67.7 1.5 %expert.3 = (f32[64,3584]{1,0:T(8,128)S(1)}, f32[1,128]{1,0:T(1,128)}) custom-call(bf16[32,2,3712]{2,1,0:T(2,128)(2,1)S(1)} %all-to-all-done.x_ref.whole_ref.refs_1_, bf16[3584,128]{1,0:T(8,128)(2,1)S(1)} %get-tuple-element.15.refs_0_.refs_2_, bf16[3584,128]{1,0:T(8,128)(2,1)S(1)} %collective-permute-done.refs_1_.refs_3_, ...), custom_call_target="tpu_custom_call" | custom-call | flops 352321536 | bytes 5505024 | tf_op jit(solution)/shard_map/expert/pallas_call | solution.py:185
  69.1 0.0 collective-permute-done.5.twin_ref
  69.1 0.4 collective-permute-done.7.refs_1_
  69.5 3.2 %collective-permute-done.6.refs_0_ = bf16[32,3584]{1,0:T(8,128)(2,1)S(1)} collective-permute-done((bf16[32,3584]{1,0:T(8,128)(2,1)S(1)}, bf16[32,3584]{1,0:T(8,128)(2,1)S(1)}, u32[]{:S(2)}, u32[]{:S(2)}) %collective-permute-start.6) | collective-permute-done | bytes 229408 | tf_op jit(solution)/shard_map/ppermute | solution.py:315
  72.7 0.2 join.1
  73.0 0.0 copy-start.1
  73.0 37.8 %all_to_all.10.rows_ref = bf16[32,2,3712]{2,1,0:T(2,128)(2,1)S(1)} all-to-all(bf16[32,2,3712]{2,1,0:T(2,128)(2,1)S(1)} %join.1), channel_id=1, replica_groups={{26,30,0,4,8,12,18,22,58,62,32,36,40,44,50,54,90,94,64,68,72,76,82,86,1..., dimensions={0} | all-to-all | bytes 950272 | tf_op jit(solution)/shard_map/all_to_all | solution.py:297
  110.8 0.0 copy-done.1
  110.8 1.0 combine.1
  (1 shorter events, 0.0 us)
Async XLA Ops:
  3.0 42.7 %all-to-all-start = ((bf16[32,2,3712]{2,1,0:T(2,128)(2,1)}), bf16[32,2,3712]{2,1,0:T(2,128)(2,1)S(1)}, u32[]{:S(2)}, u32[]{:S(2)}) async-start(bf16[32,2,3712]{2,1,0:T(2,128)(2,1)} %get-tuple-element.14), calls=%async_computation | async-start | bytes 950272 | tf_op jit(solution)/shard_map/all_to_all | solution.py:297
  20.8 33.4 %collective-permute-start = (bf16[3584,128]{1,0:T(8,128)(2,1)}, bf16[3584,128]{1,0:T(8,128)(2,1)S(1)}, u32[]{:S(2)}, u32[]{:S(2)}) collective-permute-start(bf16[3584,128]{1,0:T(8,128)(2,1)} %refs_0_.1), channel_id=1, source_target_pairs={{0,1},{1,0},{2,3},{3,2},{4,5},{5,4},{6,7},{7,6},{8,9},{9,8},{10,11... | collective-permute-start | bytes 2752520 | tf_op jit(solution)/shard_map/ppermute | solution.py:303
  22.8 31.5 %collective-permute-start.1 = (bf16[3584,128]{1,0:T(8,128)(2,1)}, bf16[3584,128]{1,0:T(8,128)(2,1)S(1)}, u32[]{:S(2)}, u32[]{:S(2)}) collective-permute-start(bf16[3584,128]{1,0:T(8,128)(2,1)} %refs_1_.1), channel_id=1, source_target_pairs={{0,1},{1,0},{2,3},{3,2},{4,5},{5,4},{6,7},{7,6},{8,9},{9,8},{10,11... | collective-permute-start | bytes 2752520 | tf_op jit(solution)/shard_map/ppermute | solution.py:303
  25.2 29.1 %collective-permute-start.2 = (bf16[128,3584]{1,0:T(8,128)(2,1)}, bf16[128,3584]{1,0:T(8,128)(2,1)S(1)}, u32[]{:S(2)}, u32[]{:S(2)}) collective-permute-start(bf16[128,3584]{1,0:T(8,128)(2,1)} %refs_2_.1), channel_id=1, source_target_pairs={{0,1},{1,0},{2,3},{3,2},{4,5},{5,4},{6,7},{7,6},{8,9},{9,8},{10,11... | collective-permute-start | bytes 2752520 | tf_op jit(solution)/shard_map/ppermute | solution.py:303
  45.7 9.8 %collective-permute-start.4 = (bf16[16,2,3712]{2,1,0:T(2,128)(2,1)S(1)}, bf16[16,2,3712]{2,1,0:T(2,128)(2,1)S(1)}, u32[]{:S(2)}, u32[]{:S(2)}) collective-permute-start(bf16[16,2,3712]{2,1,0:T(2,128)(2,1)S(1)} %get-tuple-element.20), channel_id=1, source_target_pairs={{0,2},{1,3},{2,0},{3,1},{4,6},{5,7},{6,4},{7,5},{8,10},{9,11},{10,... | collective-permute-start | bytes 712712 | tf_op jit(solution)/shard_map/ppermute | solution.py:311
  48.5 10.4 %collective-permute-start.3 = (bf16[16,2,3712]{2,1,0:T(2,128)(2,1)S(1)}, bf16[16,2,3712]{2,1,0:T(2,128)(2,1)S(1)}, u32[]{:S(2)}, u32[]{:S(2)}) collective-permute-start(bf16[16,2,3712]{2,1,0:T(2,128)(2,1)S(1)} %get-tuple-element.19), channel_id=1, source_target_pairs={{0,2},{1,3},{2,0},{3,1},{4,6},{5,7},{6,4},{7,5},{8,10},{9,11},{10,... | collective-permute-start | bytes 712712 | tf_op jit(solution)/shard_map/ppermute | solution.py:311
  51.6 1.2 %copy-start = (bf16[128,3584]{1,0:T(8,128)(2,1)S(1)}, bf16[128,3584]{1,0:T(8,128)(2,1)}, u32[]{:S(2)}) copy-start(bf16[128,3584]{1,0:T(8,128)(2,1)} %refs_2_.1) | copy-start | bytes 2752516
  59.9 9.6 %collective-permute-start.7 = (bf16[32,3584]{1,0:T(8,128)(2,1)S(1)}, bf16[32,3584]{1,0:T(8,128)(2,1)S(1)}, u32[]{:S(2)}, u32[]{:S(2)}) collective-permute-start(bf16[32,3584]{1,0:T(8,128)(2,1)S(1)} %get-tuple-element.24), channel_id=1, source_target_pairs={{0,2},{1,3},{2,0},{3,1},{4,6},{5,7},{6,4},{7,5},{8,10},{9,11},{10,... | collective-permute-start | bytes 688136 | tf_op jit(solution)/shard_map/ppermute | solution.py:315
  63.5 9.2 %collective-permute-start.6 = (bf16[32,3584]{1,0:T(8,128)(2,1)S(1)}, bf16[32,3584]{1,0:T(8,128)(2,1)S(1)}, u32[]{:S(2)}, u32[]{:S(2)}) collective-permute-start(bf16[32,3584]{1,0:T(8,128)(2,1)S(1)} %get-tuple-element.23), channel_id=1, source_target_pairs={{0,2},{1,3},{2,0},{3,1},{4,6},{5,7},{6,4},{7,5},{8,10},{9,11},{10,... | collective-permute-start | bytes 688136 | tf_op jit(solution)/shard_map/ppermute | solution.py:315
  65.8 3.4 %collective-permute-start.5 = (f32[1,128]{1,0:T(1,128)S(1)}, f32[1,128]{1,0:T(1,128)S(1)}, u32[]{:S(2)}, u32[]{:S(2)}) collective-permute-start(f32[1,128]{1,0:T(1,128)S(1)} %get-tuple-element.22.sum_ref), channel_id=1, source_target_pairs={{0,1},{1,0},{2,3},{3,2},{4,5},{5,4},{6,7},{7,6},{8,9},{9,8},{10,11... | collective-permute-start | bytes 1544 | tf_op jit(solution)/shard_map/ppermute | solution.py:318
  73.0 37.8 %copy-start.1 = (bf16[96,128]{1,0:T(8,128)(2,1)S(1)}, bf16[96,128]{1,0:T(8,128)(2,1)}, u32[]{:S(2)}) copy-start(bf16[96,128]{1,0:T(8,128)(2,1)} %get-tuple-element.25.scale_ref) | copy-start | bytes 73732

commit v6 on v5

--- a/solution.py
+++ b/solution.py
@@ -13,11 +13,16 @@
 COLS, RINGS, CORES = 4, 16, 2
 PAIRS = RINGS // 2
 CHUNKS = 2
+FIRST = 2
 F32, BF16, I32 = jnp.float32, jnp.bfloat16, jnp.int32
 
 
 def place(col, ring, core):
     return (col * RINGS + ring) * CORES + core
+
+
+def pair_of(member, side):
+    return (member + FIRST + 4 * side) & (PAIRS - 1)
 
 
 def far_groups():
@@ -27,7 +32,7 @@
             members = []
             for col in range(COLS):
                 for spot in range(PAIRS):
-                    pair = (spot + 6 + 4 * side) % PAIRS
+                    pair = pair_of(spot, side)
                     ring = 2 * pair + (side if pair < PAIRS // 2 else 1 - side)
                     members.append(place(col, ring, core))
             groups.append(members)
@@ -57,13 +62,11 @@
 
 
 def expert_of(member, side):
-    spot = member & (PAIRS - 1)
-    inner = (spot >= 2) & (spot < 6)
-    return 2 * (member >> 3) + jnp.where(inner, side, 1 - side)
+    return 2 * (member >> 3) + (pair_of(member, side) >> 2)
 
 
 def slice_of(member, side):
-    return (member & ~(PAIRS - 1)) + ((member + 6 + 4 * side) & (PAIRS - 1))
+    return (member & ~(PAIRS - 1)) + pair_of(member, side)
 
 
 def iota(shape, axis):

time: 113 us -> 110 us (0.973)
  waiting for transfers between devices: 25.8 us -> 23.1 us
  blocking collectives: 37.8 us -> 35.4 us
  starting transfers between devices: 37.7 us -> 40 us
    all_to_all x1, waiting for transfers between devices: 18.6 us -> 15.3 us  [far(): lax.all_to_all(blocks, 'exp', 0, 0, axis_index_groups=FAR, tiled=True)]
    all_to_all x1, blocking collectives: 37.8 us -> 35.4 us  [far(): lax.all_to_all(blocks, 'exp', 0, 0, axis_index_groups=FAR, tiled=True)]
    all_to_all x1, starting transfers between devices: 17.8 us -> 19.7 us  [far(): lax.all_to_all(blocks, 'exp', 0, 0, axis_index_groups=FAR, tiled=True)]
where the time goes in v6:
time: 110 us; the launch traced here: 109 us
  starting transfers between devices  40 us (36%)
  blocking collectives  35.4 us (32%)
  waiting for transfers between devices  23.1 us (21%)
  Pallas kernels  8.45 us (8%)
  local copies, waits for them, and re-layouts  1.18 us (1%)
    all_to_all x1, blocking collectives, far(): lax.all_to_all(blocks, 'exp', 0, 0, axis_index_groups=FAR, tiled=True)  35.4 us
    all_to_all x1, starting transfers between devices, far(): lax.all_to_all(blocks, 'exp', 0, 0, axis_index_groups=FAR, tiled=True)  19.7 us
    all_to_all x1, waiting for transfers between devices, far(): lax.all_to_all(blocks, 'exp', 0, 0, axis_index_groups=FAR, tiled=True)  15.3 us
    ppermute x2, starting transfers between devices, shards(): theirs.append(lax.ppermute(piece, 'exp', BESIDE))  6.29 us
    ppermute x3, starting transfers between devices, shards(): twins = tuple((lax.ppermute(w, 'exp', TWIN) for w in weights))  6.25 us
    ppermute x2, starting transfers between devices, shards(): backs.append(lax.ppermute(partial, 'exp', BESIDE))  5.84 us
    ppermute x2, waiting for transfers between devices, shards(): theirs.append(lax.ppermute(piece, 'exp', BESIDE))  4.37 us
    ppermute x2, waiting for transfers between devices, shards(): backs.append(lax.ppermute(partial, 'exp', BESIDE))  3.44 us
  transfers between devices with their start and end apart: 9, of which 5 were waited for; matrix products, arithmetic and copies ran while one was open for 0% of the time, Pallas kernels for 4%

profile of v6, /device:TPU:24, one launch (start us, length us, event | category | flops | bytes accessed | tf_op | source)
XLA Modules:
  0.0 108.9 jit_solution(133039001123950265)
XLA Ops:
  0.7 2.3 %pack.1 = (bf16[32,2,3712]{2,1,0:T(2,128)(2,1)}, bf16[96,128]{1,0:T(8,128)(2,1)}) custom-call(s32[1]{0:T(128)} %bitcast.side_ref, bf16[32,3584]{1,0:T(8,128)(2,1)} %tok_hbm.1, s32[8,32]{1,0:T(8,128)} %bitcast.3, f32[8,32]{1,0:T(8,128)} %bitcast.4), custom_call_target="tpu_custom_call" | custom-call | tf_op jit(solution)/shard_map/pack/pallas_call | solution.py:140
  3.0 19.7 %all-to-all-start = ((bf16[32,2,3712]{2,1,0:T(2,128)(2,1)}), bf16[32,2,3712]{2,1,0:T(2,128)(2,1)S(1)}, u32[]{:S(2)}, u32[]{:S(2)}) async-start(bf16[32,2,3712]{2,1,0:T(2,128)(2,1)} %get-tuple-element.14), calls=%async_computation | async-start | bytes 950272 | tf_op jit(solution)/shard_map/all_to_all | solution.py:300
  22.7 1.9 %collective-permute-start = (bf16[3584,128]{1,0:T(8,128)(2,1)}, bf16[3584,128]{1,0:T(8,128)(2,1)S(1)}, u32[]{:S(2)}, u32[]{:S(2)}) collective-permute-start(bf16[3584,128]{1,0:T(8,128)(2,1)} %refs_0_.1), channel_id=1, source_target_pairs={{0,1},{1,0},{2,3},{3,2},{4,5},{5,4},{6,7},{7,6},{8,9},{9,8},{10,11... | collective-permute-start | bytes 2752520 | tf_op jit(solution)/shard_map/ppermute | solution.py:306
  24.6 2.4 %collective-permute-start.1 = (bf16[3584,128]{1,0:T(8,128)(2,1)}, bf16[3584,128]{1,0:T(8,128)(2,1)S(1)}, u32[]{:S(2)}, u32[]{:S(2)}) collective-permute-start(bf16[3584,128]{1,0:T(8,128)(2,1)} %refs_1_.1), channel_id=1, source_target_pairs={{0,1},{1,0},{2,3},{3,2},{4,5},{5,4},{6,7},{7,6},{8,9},{9,8},{10,11... | collective-permute-start | bytes 2752520 | tf_op jit(solution)/shard_map/ppermute | solution.py:306
  27.0 1.9 %collective-permute-start.2 = (bf16[128,3584]{1,0:T(8,128)(2,1)}, bf16[128,3584]{1,0:T(8,128)(2,1)S(1)}, u32[]{:S(2)}, u32[]{:S(2)}) collective-permute-start(bf16[128,3584]{1,0:T(8,128)(2,1)} %refs_2_.1), channel_id=1, source_target_pairs={{0,1},{1,0},{2,3},{3,2},{4,5},{5,4},{6,7},{7,6},{8,9},{9,8},{10,11... | collective-permute-start | bytes 2752520 | tf_op jit(solution)/shard_map/ppermute | solution.py:306
  28.9 15.3 %all-to-all-done.x_ref.whole_ref.refs_1_ = bf16[32,2,3712]{2,1,0:T(2,128)(2,1)S(1)} async-done(((bf16[32,2,3712]{2,1,0:T(2,128)(2,1)}), bf16[32,2,3712]{2,1,0:T(2,128)(2,1)S(1)}, u32[]{:S(2)}, u32[]{:S(2)}) %all-to-all-start) | async-done | bytes 475168 | tf_op jit(solution)/shard_map/all_to_all | solution.py:300
  44.3 4.4 %collective-permute-start.4 = (bf16[16,2,3712]{2,1,0:T(2,128)(2,1)S(1)}, bf16[16,2,3712]{2,1,0:T(2,128)(2,1)S(1)}, u32[]{:S(2)}, u32[]{:S(2)}) collective-permute-start(bf16[16,2,3712]{2,1,0:T(2,128)(2,1)S(1)} %get-tuple-element.20), channel_id=1, source_target_pairs={{0,2},{1,3},{2,0},{3,1},{4,6},{5,7},{6,4},{7,5},{8,10},{9,11},{10,... | collective-permute-start | bytes 712712 | tf_op jit(solution)/shard_map/ppermute | solution.py:314
  48.7 1.9 %collective-permute-start.3 = (bf16[16,2,3712]{2,1,0:T(2,128)(2,1)S(1)}, bf16[16,2,3712]{2,1,0:T(2,128)(2,1)S(1)}, u32[]{:S(2)}, u32[]{:S(2)}) collective-permute-start(bf16[16,2,3712]{2,1,0:T(2,128)(2,1)S(1)} %get-tuple-element.19), channel_id=1, source_target_pairs={{0,2},{1,3},{2,0},{3,1},{4,6},{5,7},{6,4},{7,5},{8,10},{9,11},{10,... | collective-permute-start | bytes 712712 | tf_op jit(solution)/shard_map/ppermute | solution.py:314
  50.6 0.0 copy-start
  50.6 1.2 %copy-done = bf16[128,3584]{1,0:T(8,128)(2,1)S(1)} copy-done((bf16[128,3584]{1,0:T(8,128)(2,1)S(1)}, bf16[128,3584]{1,0:T(8,128)(2,1)}, u32[]{:S(2)}) %copy-start) | copy-done | bytes 917528
  51.8 1.5 %hold.1 = (bf16[3584,128]{1,0:T(8,128)(2,1)S(1)}, bf16[3584,128]{1,0:T(8,128)(2,1)S(1)}, bf16[128,3584]{1,0:T(8,128)(2,1)S(1)}) custom-call(bf16[3584,128]{1,0:T(8,128)(2,1)} %refs_0_.1, bf16[3584,128]{1,0:T(8,128)(2,1)} %refs_1_.1, bf16[128,3584]{1,0:T(8,128)(2,1)S(1)} %copy-done), custom_call_target="tpu_custom_call" | custom-call | tf_op jit(solution)/shard_map/hold/pallas_call | solution.py:212
  53.3 0.0 collective-permute-done.refs_1_.refs_3_
  53.3 0.0 collective-permute-done.1.refs_3_.refs_5_
  53.3 0.0 collective-permute-done.2.refs_5_.refs_7_
  53.3 2.0 %collective-permute-done.4.x_ref = bf16[16,2,3712]{2,1,0:T(2,128)(2,1)S(1)} collective-permute-done((bf16[16,2,3712]{2,1,0:T(2,128)(2,1)S(1)}, bf16[16,2,3712]{2,1,0:T(2,128)(2,1)S(1)}, u32[]{:S(2)}, u32[]{:S(2)}) %collective-permute-start.4) | collective-permute-done | bytes 237600 | tf_op jit(solution)/shard_map/ppermute | solution.py:314
  55.3 1.0 expert.4
  56.3 2.4 %collective-permute-done.3.x_ref = bf16[16,2,3712]{2,1,0:T(2,128)(2,1)S(1)} collective-permute-done((bf16[16,2,3712]{2,1,0:T(2,128)(2,1)S(1)}, bf16[16,2,3712]{2,1,0:T(2,128)(2,1)S(1)}, u32[]{:S(2)}, u32[]{:S(2)}) %collective-permute-start.3) | collective-permute-done | bytes 237600 | tf_op jit(solution)/shard_map/ppermute | solution.py:314
  58.6 1.0 expert.5
  59.6 3.0 %collective-permute-start.7 = (bf16[32,3584]{1,0:T(8,128)(2,1)S(1)}, bf16[32,3584]{1,0:T(8,128)(2,1)S(1)}, u32[]{:S(2)}, u32[]{:S(2)}) collective-permute-start(bf16[32,3584]{1,0:T(8,128)(2,1)S(1)} %get-tuple-element.24), channel_id=1, source_target_pairs={{0,2},{1,3},{2,0},{3,1},{4,6},{5,7},{6,4},{7,5},{8,10},{9,11},{10,... | collective-permute-start | bytes 688136 | tf_op jit(solution)/shard_map/ppermute | solution.py:318
  62.6 2.8 %collective-permute-start.6 = (bf16[32,3584]{1,0:T(8,128)(2,1)S(1)}, bf16[32,3584]{1,0:T(8,128)(2,1)S(1)}, u32[]{:S(2)}, u32[]{:S(2)}) collective-permute-start(bf16[32,3584]{1,0:T(8,128)(2,1)S(1)} %get-tuple-element.23), channel_id=1, source_target_pairs={{0,2},{1,3},{2,0},{3,1},{4,6},{5,7},{6,4},{7,5},{8,10},{9,11},{10,... | collective-permute-start | bytes 688136 | tf_op jit(solution)/shard_map/ppermute | solution.py:318
  65.5 1.9 %collective-permute-start.5 = (f32[1,128]{1,0:T(1,128)S(1)}, f32[1,128]{1,0:T(1,128)S(1)}, u32[]{:S(2)}, u32[]{:S(2)}) collective-permute-start(f32[1,128]{1,0:T(1,128)S(1)} %get-tuple-element.22.sum_ref), channel_id=1, source_target_pairs={{0,1},{1,0},{2,3},{3,2},{4,5},{5,4},{6,7},{7,6},{8,9},{9,8},{10,11... | collective-permute-start | bytes 1544 | tf_op jit(solution)/shard_map/ppermute | solution.py:321
  67.4 1.5 %expert.3 = (f32[64,3584]{1,0:T(8,128)S(1)}, f32[1,128]{1,0:T(1,128)}) custom-call(bf16[32,2,3712]{2,1,0:T(2,128)(2,1)S(1)} %all-to-all-done.x_ref.whole_ref.refs_1_, bf16[3584,128]{1,0:T(8,128)(2,1)S(1)} %get-tuple-element.15.refs_0_.refs_2_, bf16[3584,128]{1,0:T(8,128)(2,1)S(1)} %collective-permute-done.refs_1_.refs_3_, ...), custom_call_target="tpu_custom_call" | custom-call | flops 352321536 | bytes 5505024 | tf_op jit(solution)/shard_map/expert/pallas_call | solution.py:188
  68.9 0.0 collective-permute-done.5.twin_ref
  68.9 1.0 collective-permute-done.7.refs_1_
  69.8 2.5 %collective-permute-done.6.refs_0_ = bf16[32,3584]{1,0:T(8,128)(2,1)S(1)} collective-permute-done((bf16[32,3584]{1,0:T(8,128)(2,1)S(1)}, bf16[32,3584]{1,0:T(8,128)(2,1)S(1)}, u32[]{:S(2)}, u32[]{:S(2)}) %collective-permute-start.6) | collective-permute-done | bytes 229408 | tf_op jit(solution)/shard_map/ppermute | solution.py:318
  72.3 0.2 join.1
  72.5 0.0 copy-start.1
  72.5 35.4 %all_to_all.10.rows_ref = bf16[32,2,3712]{2,1,0:T(2,128)(2,1)S(1)} all-to-all(bf16[32,2,3712]{2,1,0:T(2,128)(2,1)S(1)} %join.1), channel_id=1, replica_groups={{8,12,18,22,26,30,0,4,40,44,50,54,58,62,32,36,72,76,82,86,90,94,64,68,1..., dimensions={0} | all-to-all | bytes 950272 | tf_op jit(solution)/shard_map/all_to_all | solution.py:300
  107.9 0.0 copy-done.1
  107.9 1.0 combine.1
  (1 shorter events, 0.0 us)
Async XLA Ops:
  3.0 41.3 %all-to-all-start = ((bf16[32,2,3712]{2,1,0:T(2,128)(2,1)}), bf16[32,2,3712]{2,1,0:T(2,128)(2,1)S(1)}, u32[]{:S(2)}, u32[]{:S(2)}) async-start(bf16[32,2,3712]{2,1,0:T(2,128)(2,1)} %get-tuple-element.14), calls=%async_computation | async-start | bytes 950272 | tf_op jit(solution)/shard_map/all_to_all | solution.py:300
  22.7 30.6 %collective-permute-start = (bf16[3584,128]{1,0:T(8,128)(2,1)}, bf16[3584,128]{1,0:T(8,128)(2,1)S(1)}, u32[]{:S(2)}, u32[]{:S(2)}) collective-permute-start(bf16[3584,128]{1,0:T(8,128)(2,1)} %refs_0_.1), channel_id=1, source_target_pairs={{0,1},{1,0},{2,3},{3,2},{4,5},{5,4},{6,7},{7,6},{8,9},{9,8},{10,11... | collective-permute-start | bytes 2752520 | tf_op jit(solution)/shard_map/ppermute | solution.py:306
  24.6 28.7 %collective-permute-start.1 = (bf16[3584,128]{1,0:T(8,128)(2,1)}, bf16[3584,128]{1,0:T(8,128)(2,1)S(1)}, u32[]{:S(2)}, u32[]{:S(2)}) collective-permute-start(bf16[3584,128]{1,0:T(8,128)(2,1)} %refs_1_.1), channel_id=1, source_target_pairs={{0,1},{1,0},{2,3},{3,2},{4,5},{5,4},{6,7},{7,6},{8,9},{9,8},{10,11... | collective-permute-start | bytes 2752520 | tf_op jit(solution)/shard_map/ppermute | solution.py:306
  27.0 26.3 %collective-permute-start.2 = (bf16[128,3584]{1,0:T(8,128)(2,1)}, bf16[128,3584]{1,0:T(8,128)(2,1)S(1)}, u32[]{:S(2)}, u32[]{:S(2)}) collective-permute-start(bf16[128,3584]{1,0:T(8,128)(2,1)} %refs_2_.1), channel_id=1, source_target_pairs={{0,1},{1,0},{2,3},{3,2},{4,5},{5,4},{6,7},{7,6},{8,9},{9,8},{10,11... | collective-permute-start | bytes 2752520 | tf_op jit(solution)/shard_map/ppermute | solution.py:306
  44.3 11.0 %collective-permute-start.4 = (bf16[16,2,3712]{2,1,0:T(2,128)(2,1)S(1)}, bf16[16,2,3712]{2,1,0:T(2,128)(2,1)S(1)}, u32[]{:S(2)}, u32[]{:S(2)}) collective-permute-start(bf16[16,2,3712]{2,1,0:T(2,128)(2,1)S(1)} %get-tuple-element.20), channel_id=1, source_target_pairs={{0,2},{1,3},{2,0},{3,1},{4,6},{5,7},{6,4},{7,5},{8,10},{9,11},{10,... | collective-permute-start | bytes 712712 | tf_op jit(solution)/shard_map/ppermute | solution.py:314
  48.7 10.0 %collective-permute-start.3 = (bf16[16,2,3712]{2,1,0:T(2,128)(2,1)S(1)}, bf16[16,2,3712]{2,1,0:T(2,128)(2,1)S(1)}, u32[]{:S(2)}, u32[]{:S(2)}) collective-permute-start(bf16[16,2,3712]{2,1,0:T(2,128)(2,1)S(1)} %get-tuple-element.19), channel_id=1, source_target_pairs={{0,2},{1,3},{2,0},{3,1},{4,6},{5,7},{6,4},{7,5},{8,10},{9,11},{10,... | collective-permute-start | bytes 712712 | tf_op jit(solution)/shard_map/ppermute | solution.py:314
  50.6 1.2 %copy-start = (bf16[128,3584]{1,0:T(8,128)(2,1)S(1)}, bf16[128,3584]{1,0:T(8,128)(2,1)}, u32[]{:S(2)}) copy-start(bf16[128,3584]{1,0:T(8,128)(2,1)} %refs_2_.1) | copy-start | bytes 2752516
  59.6 10.2 %collective-permute-start.7 = (bf16[32,3584]{1,0:T(8,128)(2,1)S(1)}, bf16[32,3584]{1,0:T(8,128)(2,1)S(1)}, u32[]{:S(2)}, u32[]{:S(2)}) collective-permute-start(bf16[32,3584]{1,0:T(8,128)(2,1)S(1)} %get-tuple-element.24), channel_id=1, source_target_pairs={{0,2},{1,3},{2,0},{3,1},{4,6},{5,7},{6,4},{7,5},{8,10},{9,11},{10,... | collective-permute-start | bytes 688136 | tf_op jit(solution)/shard_map/ppermute | solution.py:318
  62.6 9.7 %collective-permute-start.6 = (bf16[32,3584]{1,0:T(8,128)(2,1)S(1)}, bf16[32,3584]{1,0:T(8,128)(2,1)S(1)}, u32[]{:S(2)}, u32[]{:S(2)}) collective-permute-start(bf16[32,3584]{1,0:T(8,128)(2,1)S(1)} %get-tuple-element.23), channel_id=1, source_target_pairs={{0,2},{1,3},{2,0},{3,1},{4,6},{5,7},{6,4},{7,5},{8,10},{9,11},{10,... | collective-permute-start | bytes 688136 | tf_op jit(solution)/shard_map/ppermute | solution.py:318
  65.5 3.4 %collective-permute-start.5 = (f32[1,128]{1,0:T(1,128)S(1)}, f32[1,128]{1,0:T(1,128)S(1)}, u32[]{:S(2)}, u32[]{:S(2)}) collective-permute-start(f32[1,128]{1,0:T(1,128)S(1)} %get-tuple-element.22.sum_ref), channel_id=1, source_target_pairs={{0,1},{1,0},{2,3},{3,2},{4,5},{5,4},{6,7},{7,6},{8,9},{9,8},{10,11... | collective-permute-start | bytes 1544 | tf_op jit(solution)/shard_map/ppermute | solution.py:321
  72.5 35.4 %copy-start.1 = (bf16[96,128]{1,0:T(8,128)(2,1)S(1)}, bf16[96,128]{1,0:T(8,128)(2,1)}, u32[]{:S(2)}) copy-start(bf16[96,128]{1,0:T(8,128)(2,1)} %get-tuple-element.25.scale_ref) | copy-start | bytes 73732
